TPU v7x, 32 devices: a whole 2x2x4 slice. The times are simulated.
32 devices in a mesh: gx: 2 (over y), gy: 4 (over z), gz: 4 (over x, core).
Axes of the slice: x: 2, y: 2, z: 4, core: 2. Of those that a mesh axis runs over, the one named last changes fastest.
Arguments:
- couplings: float32 [18, 16, 32, 512], P(None, 'gx', 'gy', 'gz'), may hold values from 0.05 to 2
- diagonal: float32 [3, 16, 32, 512], P(None, 'gx', 'gy', 'gz'), may hold values from 0.01 to 0.1
- right_side: float32 [3, 16, 32, 512], P(None, 'gx', 'gy', 'gz'), may hold values from -6 to 6
- guess: float32 [3, 16, 32, 512], P(None, 'gx', 'gy', 'gz'), may hold values from -4 to 4
Outputs:
- solution: float32 [3, 16, 32, 512], P(None, 'gx', 'gy', 'gz')
All inputs are finite; a program needn't handle non-finite values.
Results may differ from a plain program's by a relative error of at most 0.00011.
Values sent between devices are 32-bit elements; how exact they have to be, the bound alone decides.
A program may use at most 128 MiB of HBM per device.

v0:
```python
import functools

import jax
import jax.numpy as jnp
from jax import lax
from jax.experimental import pallas as pl
from jax.experimental.pallas import tpu as pltpu
from jax.sharding import PartitionSpec as P

SWEEPS = 2
COARSE_SWEEPS = 8
DAMP = 0.8
EQ = 3
MESH = pl.DeviceIdType.MESH
HIGH = lax.Precision.HIGHEST


def roll(value, shift, axis):
    size = value.shape[axis]
    shift = shift % size
    return value if shift == 0 else pltpu.roll(value, shift, axis)


def iota(shape, axis):
    return lax.broadcasted_iota(jnp.int32, shape, axis)


def kernel(
    dims, cores, w_ref, d_ref, b_ref, g_ref, out_ref,
    field, halo_x, halo_y, pack_s, pack_r, tot0, c0, w1, tot1, c1, b1,
    wsend, wall, bsend, ball, e2, lines,
    s_sem, r_sem, ws_sem, wr_sem, bs_sem, br_sem, l_sem,
):
    ngx, ngy, ngz = dims
    nx, ny, nz = g_ref.shape[1:]
    qx, qy, qz = nx // 4, ny // 4, nz // 4
    rows = ngx * ngy
    nX = ngz // cores
    gx, gy, gz = lax.axis_index("gx"), lax.axis_index("gy"), lax.axis_index("gz")
    X, core = gz // cores, gz % cores
    row = gy * ngx + gx
    axes = (("gx", gx, ngx), ("gy", gy, ngy), ("gz", gz, ngz))

    def device(name, index):
        here = {"gx": gx, "gy": gy, "gz": gz}
        here[name] = index
        return (here["gx"], here["gy"], here["gz"])

    barrier = pltpu.get_barrier_semaphore()
    close = ngy <= 4 and ngz <= 4
    awaited = 0
    for name, index, count in axes:
        if close and name != "gx":
            for step in (-1, 1):
                @pl.when((index + step >= 0) & (index + step < count))
                def _():
                    pl.semaphore_signal(
                        barrier, inc=1, device_id=device(name, jnp.clip(index + step, 0, count - 1)),
                        device_id_type=MESH,
                    )
            awaited = awaited + (index > 0).astype(jnp.int32) + (index < count - 1).astype(jnp.int32)
        else:
            for step in range(1, count):
                pl.semaphore_signal(
                    barrier, inc=1, device_id=device(name, (index + step) % count), device_id_type=MESH
                )
            awaited = awaited + (count - 1)

    rounds = field.shape[0]
    for name, index, count in axes:
        for side in range(2):
            @pl.when(index == (0 if side == 0 else count - 1))
            def _():
                for r in range(rounds):
                    if name == "gx":
                        halo_x[r, side] = jnp.zeros(halo_x.shape[2:], jnp.float32)
                    elif name == "gy":
                        lo = 0 if side == 0 else ny // 2
                        halo_y[r, :, :, lo : lo + ny // 2] = jnp.zeros(
                            (EQ, nx, ny // 2, nz), jnp.float32
                        )
                    else:
                        pack_r[r, side] = jnp.zeros(pack_r.shape[2:], jnp.float32)

    pl.semaphore_wait(barrier, awaited)

    lane2 = iota((ny, nz), 1)

    def copies(r, n, s):
        src = g_ref if r == 0 else field.at[r]
        made = []
        for side in range(2):
            other = 1 - side
            for place, (name, index, count) in enumerate(axes):
                if name == "gx":
                    a = src.at[:, 0 if side == 0 else n - 1]
                    z = halo_x.at[r, other]
                elif name == "gy":
                    a = src.at[:, 0:n, pl.ds(0 if side == 0 else ny - s, s)]
                    z = halo_y.at[r, :, 0:n, pl.ds(ny - s if side == 0 else 0, s)]
                else:
                    a = pack_s.at[r, side]
                    z = pack_r.at[r, other]
                target = index - 1 if side == 0 else index + 1
                has_target = index > 0 if side == 0 else index < count - 1
                has_source = index < count - 1 if side == 0 else index > 0
                slot = 2 * place + side
                made.append((
                    pltpu.make_async_remote_copy(
                        src_ref=a, dst_ref=z,
                        send_sem=s_sem.at[r, slot], recv_sem=r_sem.at[r, slot],
                        device_id=device(name, jnp.clip(target, 0, count - 1)),
                        device_id_type=MESH,
                    ),
                    has_target, has_source, name,
                ))
        return made

    def send(r, value, n, s):
        made = copies(r, n, s)
        if r > 0:
            for e in range(EQ):
                field[r, e, 0:n] = value[e]
        for copy, has_target, _, name in made:
            if name != "gz":
                @pl.when(has_target)
                def _():
                    copy.start()
        low = jnp.zeros((ny, nz), jnp.float32)
        high = jnp.zeros((ny, nz), jnp.float32)
        for e in range(EQ):
            for i in range(n):
                here = lane2 == e * n + i
                low = jnp.where(here, jnp.broadcast_to(value[e][i, :, 0:1], (ny, nz)), low)
                high = jnp.where(here, jnp.broadcast_to(value[e][i, :, nz - 1 : nz], (ny, nz)), high)
        pack_s[r, 0] = low
        pack_s[r, 1] = high
        for copy, has_target, _, name in made:
            if name == "gz":
                @pl.when(has_target)
                def _():
                    copy.start()

    def receive(r, n, s):
        for copy, _, has_source, _ in copies(r, n, s):
            @pl.when(has_source)
            def _():
                copy.wait_recv()

    def before(v, e, n, s, weight, base, scale):
        shape = (n, ny, nz)
        y, z = iota(shape, 1), iota(shape, 2)
        edge = jnp.zeros((1, ny, nz), jnp.float32)
        near = [
            jnp.concatenate([v[1:], edge], axis=0),
            jnp.concatenate([edge, v[:-1]], axis=0),
            jnp.where(y >= ny - s, 0.0, roll(v, -s, 1)),
            jnp.where(y < s, 0.0, roll(v, s, 1)),
            jnp.where(z >= nz - s, 0.0, roll(v, -s, 2)),
            jnp.where(z < s, 0.0, roll(v, s, 2)),
        ]
        w = [weight(e, k) for k in range(6)]
        total = w[0] * near[0]
        for k in range(1, 6):
            total = total + w[k] * near[k]
        wy = jnp.where(y >= ny - s, w[2], jnp.where(y < s, w[3], 0.0))
        wz = jnp.where(z >= nz - s, w[4], jnp.where(z < s, w[5], 0.0))
        up, down = w[0][n - 1], w[1][0]
        if scale is not None:
            total, wy, wz = scale * total, scale * wy, scale * wz
            up, down = scale[n - 1] * up, scale[0] * down
        return base + total, up, down, wy, wz

    def after(r, e, n, s, ready):
        total, up, down, wy, wz = ready
        shape = (n, ny, nz)
        y, z = iota(shape, 1), iota(shape, 2)
        low = pack_r[r, 0]
        high = pack_r[r, 1]
        zl = jnp.stack([jnp.broadcast_to(low[:, e * n + i : e * n + i + 1], (ny, nz)) for i in range(n)])
        zh = jnp.stack([jnp.broadcast_to(high[:, e * n + i : e * n + i + 1], (ny, nz)) for i in range(n)])
        hy = jnp.where((y < s) | (y >= ny - s), halo_y[r, e, 0:n], 0.0)
        total = total + wy * hy + wz * jnp.where(z < s, zl, zh)
        first = total[0] + down * halo_x[r, 0, e]
        last = total[n - 1] + up * halo_x[r, 1, e]
        return jnp.concatenate([first[None], total[1 : n - 1], last[None]], axis=0)

    def coarsen(a, s):
        n = a.shape[0]
        a = jnp.stack([a[2 * i] + a[2 * i + 1] for i in range(n // 2)])
        y, z = iota(a.shape, 1), iota(a.shape, 2)
        a = a + jnp.where((y // s) % 2 == 0, roll(a, -s, 1), roll(a, s, 1))
        a = a + jnp.where((z // s) % 2 == 0, roll(a, -s, 2), roll(a, s, 2))
        return a * 0.125

    def spread(a):
        return jnp.stack([a[i // 2] for i in range(2 * a.shape[0])])

    def weight0(e, k):
        return w_ref[6 * e + k]

    def weight1(e, k):
        return w1[6 * e + k]

    source = iota((nz, nz), 0)
    target = iota((nz, nz), 1)
    squeeze = jnp.where(source == 4 * (target % qz), 1.0, 0.0).astype(jnp.float32)

    def to_rows(a):
        m = a.shape[0]
        c = jnp.dot(a.reshape(m * qx * ny, nz), squeeze, precision=HIGH,
                    preferred_element_type=jnp.float32).reshape(m, qx, ny, nz)
        shape = (m, ny, nz)
        lane = iota(shape, 2)
        got = jnp.zeros(shape, jnp.float32)
        for x in range(qx):
            for y in range(qy):
                part = roll(c[:, x], -4 * y, 1)
                got = jnp.where(lane // qz == x * qy + y, part, got)
        return got

    def own(small, whole, sem):
        return pltpu.make_async_copy(
            small.at[:, pl.ds(0, 1)], whole.at[X, core, :, pl.ds(row, 1)], sem
        )

    def stage(number, small, whole, ss, rs):
        made = []
        if number == 0:
            for step in range(1, ngx):
                made.append((small.at[:, pl.ds(0, 1)], whole.at[X, core, :, pl.ds(row, 1)],
                             step, device("gx", (gx + step) % ngx)))
        elif number == 1:
            block = whole.at[X, core, :, pl.ds(gy * ngx, ngx)]
            for step in range(1, ngy):
                made.append((block, block, step, device("gy", (gy + step) % ngy)))
        elif number == 2:
            block = whole.at[X, core]
            for step in range(1, nX):
                made.append((block, block, step, device("gz", ((X + step) % nX) * cores + core)))
        else:
            block = whole.at[:, core]
            for step in range(1, cores):
                made.append((block, block, step, device("gz", X * cores + (core + step) % cores)))
        return [
            pltpu.make_async_remote_copy(
                src_ref=a, dst_ref=z, send_sem=ss.at[number, step], recv_sem=rs.at[number, step],
                device_id=where, device_id_type=MESH,
            )
            for a, z, step, where in made
        ]

    wargs = (wsend, wall, ws_sem, wr_sem)

    def everyone():
        made = []
        for az in range(ngz):
            for ay in range(ngy):
                for ax in range(ngx):
                    if ax + ay + az == 0:
                        continue
                    made.append(pltpu.make_async_remote_copy(
                        src_ref=bsend.at[:, pl.ds(0, 1)],
                        dst_ref=ball.at[X, core, :, pl.ds(row, 1)],
                        send_sem=bs_sem, recv_sem=br_sem,
                        device_id=((gx + ax) % ngx, (gy + ay) % ngy, (gz + az) % ngz),
                        device_id_type=MESH,
                    ))
        return made

    def start(number, args):
        for copy in stage(number, *args):
            copy.start()

    def finish(number, args):
        for copy in stage(number, *args):
            copy.wait_recv()

    v = [g_ref[e] for e in range(EQ)]
    send(0, v, nx, 1)
    for e in range(EQ):
        total = d_ref[e]
        for k in range(6):
            total = total + w_ref[6 * e + k]
        tot0[e] = total
        c0[e] = DAMP / total
        total = coarsen(d_ref[e], 1)
        wsend_d = coarsen(total, 2)
        for k in range(6):
            w = 0.25 * coarsen(w_ref[6 * e + k], 1)
            w1[6 * e + k] = w
            total = total + w
            wsend[6 * e + k] = to_rows((0.25 * coarsen(w, 2))[None])[0]
        wsend[6 * EQ + e] = to_rows(wsend_d[None])[0]
        tot1[e] = total
        c1[e] = DAMP / total
    own(wsend, wall, l_sem.at[0]).start()
    start(0, wargs)

    keep = 1.0 - DAMP

    def apply(r, v, n, s, weight, base, scale):
        ready = [
            before(v[e], e, n, s, weight, base(e), None if scale is None else scale[e])
            for e in range(EQ)
        ]
        if r != 5:
            receive(r, n, s)
        return [after(r, e, n, s, ready[e]) for e in range(EQ)]

    def smooth0(r, v):
        return apply(r, v, nx, 1, weight0, lambda e: keep * v[e] + c0[e] * b_ref[e], c0)

    def smooth1(r, v):
        return apply(r, v, nx // 2, 2, weight1, lambda e: keep * v[e] + c1[e] * b1[e], c1)

    v = smooth0(0, v)
    send(1, v, nx, 1)
    v = smooth0(1, v)
    own(wsend, wall, l_sem.at[0]).wait()
    finish(0, wargs)
    send(2, v, nx, 1)
    start(1, wargs)
    u = []
    rest = apply(2, v, nx, 1, weight0, lambda e: b_ref[e] - tot0[e] * v[e], None)
    for e in range(EQ):
        b = coarsen(rest[e], 1)
        b1[e] = b
        u.append(c1[e] * b)
    half = nx // 2
    send(3, u, half, 2)
    u = smooth1(3, u)
    finish(1, wargs)
    send(4, u, half, 2)
    start(2, wargs)
    rest = apply(4, u, half, 2, weight1, lambda e: b1[e] - tot1[e] * u[e], None)
    bsend[...] = to_rows(jnp.stack([coarsen(rest[e], 2) for e in range(EQ)]))
    for copy in reversed(everyone()):
        copy.start()
    own(bsend, ball, br_sem).start()
    finish(2, wargs)
    start(3, wargs)
    finish(3, wargs)

    shape = (ngz, rows, nz)
    r_i, l_i = iota(shape, 1), iota(shape, 2)
    g_i = iota(shape, 0)
    zi, yi, xi = l_i % qz, (l_i // qz) % qy, l_i // (qz * qy)
    gyi, gxi = r_i // ngx, r_i % ngx
    inside = [
        ~((xi == qx - 1) & (gxi == ngx - 1)), ~((xi == 0) & (gxi == 0)),
        ~((yi == qy - 1) & (gyi == ngy - 1)), ~((yi == 0) & (gyi == 0)),
        ~((zi == qz - 1) & (g_i == ngz - 1)), ~((zi == 0) & (g_i == 0)),
    ]

    def whole(ref, index):
        return ref[:, :, index].reshape(shape)

    def next_of(v):
        return jnp.concatenate([v[1:], v[:1]], axis=0)

    def prev_of(v):
        return jnp.concatenate([v[-1:], v[:-1]], axis=0)

    def near2(v):
        sy, sx = qz, qz * qy
        return [
            jnp.where(xi == qx - 1, roll(roll(v, (qx - 1) * sx, 2), -1, 1), roll(v, -sx, 2)),
            jnp.where(xi == 0, roll(roll(v, -(qx - 1) * sx, 2), 1, 1), roll(v, sx, 2)),
            jnp.where(yi == qy - 1, roll(roll(v, (qy - 1) * sy, 2), -ngx, 1), roll(v, -sy, 2)),
            jnp.where(yi == 0, roll(roll(v, -(qy - 1) * sy, 2), ngx, 1), roll(v, sy, 2)),
            jnp.where(zi == qz - 1, roll(next_of(v), qz - 1, 2), roll(v, -1, 2)),
            jnp.where(zi == 0, roll(prev_of(v), -(qz - 1), 2), roll(v, 1, 2)),
        ]

    def dot_near(weights, near):
        total = weights[0] * near[0]
        for k in range(1, 6):
            total = total + weights[k] * near[k]
        return total

    def pair(a):
        sy, sx = qz, qz * qy
        a = a + jnp.where(xi % 2 == 0, roll(a, -sx, 2), roll(a, sx, 2))
        a = a + jnp.where(yi % 2 == 0, roll(a, -sy, 2), roll(a, sy, 2))
        a = a + jnp.where(zi % 2 == 0, roll(a, -1, 2), roll(a, 1, 2))
        return a * 0.125

    groups = qx * qy
    tiles = ngz // groups
    shape3 = (tiles, rows, nz)
    r3, l3, t3 = iota(shape3, 1), iota(shape3, 2), iota(shape3, 0)
    inside3 = [
        r3 % ngx < ngx - 1, r3 % ngx > 0, r3 // ngx < ngy - 1, r3 // ngx > 0,
        ~((l3 >= nz - 2) & (t3 == tiles - 1)), ~((l3 < 2) & (t3 == 0)),
    ]

    def join(a):
        a = a.reshape(tiles, groups, rows, nz)
        got = a[:, 0]
        for j in range(1, groups):
            got = jnp.where(l3 // qz == j, a[:, j], got)
        return got

    def part(a):
        parts = []
        for j in range(groups):
            mine = jnp.where(l3 // qz == j, a, 0.0)
            size = qz
            while size < nz:
                mine = mine + roll(mine, size, 2)
                size *= 2
            parts.append(mine)
        return jnp.stack(parts, axis=1).reshape(shape)

    def near3(v):
        if tiles == 1:
            up, down = roll(v, -2, 2), roll(v, 2, 2)
        else:
            up = jnp.where(l3 >= nz - 2, roll(next_of(v), -2, 2), roll(v, -2, 2))
            down = jnp.where(l3 < 2, roll(prev_of(v), 2, 2), roll(v, 2, 2))
        return [roll(v, -1, 1), roll(v, 1, 1), roll(v, -ngx, 1), roll(v, ngx, 1), up, down]

    w2, t2, w3, t3s = [], [], [], []
    for e in range(EQ):
        plain = [whole(wall, 6 * e + k) for k in range(6)]
        d2 = whole(wall, 6 * EQ + e)
        total = d2
        for k in range(6):
            total = total + plain[k]
        t2.append(total)
        w2.append([jnp.where(inside[k], plain[k], 0.0) for k in range(6)])
        plain3 = [0.25 * join(pair(plain[k])) for k in range(6)]
        total = join(pair(d2))
        for k in range(6):
            total = total + plain3[k]
        t3s.append(total)
        w3.append([jnp.where(inside3[k], plain3[k], 0.0) for k in range(6)])
    c2 = [DAMP / t for t in t2]
    c3 = [DAMP / t for t in t3s]

    pltpu.make_async_copy(ball, ball, br_sem).wait()

    every = range(EQ)
    rhs = [whole(ball, e) for e in every]

    def smooth2(v):
        return [keep * v[e] + c2[e] * (rhs[e] + dot_near(w2[e], near2(v[e]))) for e in every]

    v2 = [c2[e] * rhs[e] for e in every]
    for step in range(SWEEPS - 1):
        v2 = smooth2(v2)
    rest = [rhs[e] - t2[e] * v2[e] + dot_near(w2[e], near2(v2[e])) for e in every]
    rhs3 = [join(pair(rest[e])) for e in every]
    v3 = [c3[e] * rhs3[e] for e in every]
    for step in range(COARSE_SWEEPS - 1):
        v3 = [keep * v3[e] + c3[e] * (rhs3[e] + dot_near(w3[e], near3(v3[e]))) for e in every]
    v2 = [v2[e] + part(v3[e]) for e in every]
    for step in range(SWEEPS):
        v2 = smooth2(v2)
    for e in every:
        e2[e] = v2[e]

    wide = groups * nz
    source = iota((nz, wide), 0)
    target = iota((nz, wide), 1)
    widen = jnp.where(source == (target // nz) * qz + (target % nz) // 4, 1.0, 0.0).astype(jnp.float32)
    around = [(gx, gy, gz, None)]
    for axis, index, count in ((0, gx, ngx), (1, gy, ngy), (2, gz, ngz)):
        for step in (-1, 1):
            at = [gx, gy, gz]
            at[axis] = jnp.clip(index + step, 0, count - 1)
            has = index > 0 if step < 0 else index < count - 1
            around.append((at[0], at[1], at[2], has))
    for e in range(EQ):
        for j, (ax, ay, az, has) in enumerate(around):
            line = e2[e, az, pl.ds(ay * ngx + ax, 1), :]
            if has is not None:
                line = jnp.where(has, line, 0.0)
            lines[e * 7 + j : e * 7 + j + 1, :] = line
    for j in range(EQ * 7, lines.shape[0]):
        lines[j : j + 1, :] = jnp.zeros((1, nz), jnp.float32)
    back = jnp.dot(lines[...], widen, precision=HIGH, preferred_element_type=jnp.float32)
    ysel = iota((ny, nz), 0) // 4

    def strip(e, j, x, y):
        col = (x * qy + y) * nz
        return jnp.broadcast_to(back[e * 7 + j : e * 7 + j + 1, col : col + nz], (ny, nz))

    def plane(e, j, x):
        got = strip(e, j, x, 0)
        for y in range(1, qy):
            got = jnp.where(ysel == y, strip(e, j, x, y), got)
        return got

    low, high = pack_r[4, 0], pack_r[4, 1]
    for e in range(EQ):
        halo_x[5, 0, e] = halo_x[4, 0, e] + plane(e, 1, qx - 1)
        halo_x[5, 1, e] = halo_x[4, 1, e] + plane(e, 2, 0)
        for x in range(qx):
            edge = jnp.where(ysel < qy // 2, strip(e, 3, x, qy - 1), strip(e, 4, x, 0))
            below, above = plane(e, 5, x), plane(e, 6, x)
            for i in (2 * x, 2 * x + 1):
                halo_y[5, e, i] = halo_y[4, e, i] + edge
                here = lane2 == e * half + i
                low = jnp.where(here, low + jnp.broadcast_to(below[:, nz - 1 : nz], (ny, nz)), low)
                high = jnp.where(here, high + jnp.broadcast_to(above[:, 0:1], (ny, nz)), high)
        u[e] = u[e] + spread(jnp.stack([plane(e, 0, x) for x in range(qx)]))
    pack_r[5, 0] = low
    pack_r[5, 1] = high
    u = smooth1(5, u)
    send(6, u, half, 2)
    u = smooth1(6, u)
    v = [field[2, e] + spread(u[e]) for e in range(EQ)]
    send(7, v, nx, 1)
    v = smooth0(7, v)
    send(8, v, nx, 1)
    v = smooth0(8, v)
    for e in range(EQ):
        out_ref[e] = v[e]

    for r in range(rounds):
        if r == 5:
            continue
        n, s = (half, 2) if 3 <= r <= 6 else (nx, 1)
        for copy, has_target, _, _ in copies(r, n, s):
            @pl.when(has_target)
            def _():
                copy.wait_send()
    for number in range(4):
        for copy in stage(number, *wargs):
            copy.wait_send()
    for copy in everyone():
        copy.wait_send()


def per_device(dims, cores, couplings, diagonal, right_side, guess):
    ngx, ngy, ngz = dims
    brick = guess.shape[1:]
    nx, ny, nz = brick
    half = nx // 2
    rows = ngx * ngy
    nX = ngz // cores
    rounds = 9
    peers = max(ngx, ngy, nX, cores)
    f32 = jnp.float32
    vmem = pltpu.VMEM
    dma = pltpu.SemaphoreType.DMA
    return pl.pallas_call(
        functools.partial(kernel, dims, cores),
        out_shape=jax.ShapeDtypeStruct(guess.shape, f32),
        in_specs=[pl.BlockSpec(memory_space=vmem)] * 4,
        out_specs=pl.BlockSpec(memory_space=vmem),
        scratch_shapes=[
            vmem((rounds, EQ) + brick, f32),
            vmem((rounds, 2, EQ, ny, nz), f32),
            vmem((rounds, EQ) + brick, f32),
            vmem((rounds, 2, ny, nz), f32),
            vmem((rounds, 2, ny, nz), f32),
            vmem((EQ,) + brick, f32),
            vmem((EQ,) + brick, f32),
            vmem((6 * EQ, half, ny, nz), f32),
            vmem((EQ, half, ny, nz), f32),
            vmem((EQ, half, ny, nz), f32),
            vmem((EQ, half, ny, nz), f32),
            vmem((7 * EQ, ny, nz), f32),
            vmem((nX, cores, 7 * EQ, rows, nz), f32),
            vmem((EQ, ny, nz), f32),
            vmem((nX, cores, EQ, rows, nz), f32),
            vmem((EQ, ngz, rows, nz), f32),
            vmem((-(-EQ * 7 // 8) * 8, nz), f32),
            dma((rounds, 6)),
            dma((rounds, 6)),
            dma((4, peers)),
            dma((4, peers)),
            dma,
            dma,
            dma((1,)),
        ],
        compiler_params=pltpu.CompilerParams(
            collective_id=0, has_side_effects=True, vmem_limit_bytes=60 * 1024 * 1024
        ),
    )(couplings, diagonal, right_side, guess)


def solution(mesh):
    dims = (mesh.shape["gx"], mesh.shape["gy"], mesh.shape["gz"])
    cores = 2 if dims[2] % 2 == 0 else 1
    spec = P(None, "gx", "gy", "gz")
    return jax.shard_map(
        functools.partial(per_device, dims, cores),
        mesh=mesh,
        in_specs=(spec,) * 4,
        out_specs=spec,
        check_vma=False,
    )
```

profile of v0, /device:TPU:0, one launch (start us, length us, event | category | flops | bytes accessed | tf_op | source)
XLA Modules:
  0.0 39.1 jit_solution(10674775428747800221)
XLA Ops:
  0.0 37.5 %shard_map.46 = f32[3,8,8,128]{3,2,1,0:T(8,128)} custom-call(f32[18,8,8,128]{3,2,1,0:T(8,128)} %w_ref.1, f32[3,8,8,128]{3,2,1,0:T(8,128)} %d_ref.1, f32[3,8,8,128]{3,2,1,0:T(8,128)} %b_ref.1, f32[3,8,8,128]{3,2,1,0:T(8,128)} %g_ref.1), custom_call_target="tpu_custom_call" | custom-call | tf_op jit(solution)/shard_map/pallas_call | solution.py:549
  37.5 1.5 %copy.6 = f32[3,8,8,128]{3,2,1,0:T(8,128)} copy(f32[3,8,8,128]{3,2,1,0:T(8,128)} %shard_map.46) | data formatting | bytes 196608
where the time goes:
time: 39.2 us; the launch traced here: 39.1 us
  Pallas kernels  37.5 us (96%)
  local copies, waits for them, and re-layouts  1.54 us (4%)
    pallas_call x1, Pallas kernels, per_device(): pl.pallas_call(functools.partial(kernel, dims, cores), out_shape=jax.Shap...  37.5 us
    unnamed x1, local copies, waits for them, and re-layouts  1.54 us

commit v1 on v0

--- a/solution.py
+++ b/solution.py
@@ -26,10 +26,10 @@
 
 
 def kernel(
-    dims, cores, w_ref, d_ref, b_ref, g_ref, out_ref,
-    field, halo_x, halo_y, pack_s, pack_r, tot0, c0, w1, tot1, c1, b1,
+    dims, cores, w_hbm, d_hbm, b_hbm, g_hbm, out_ref,
+    w_ref, d_ref, b_ref, g_ref, field, halo_x, halo_y, pack_s, pack_r, tot0, c0, w1, tot1, c1, b1,
     wsend, wall, bsend, ball, e2, lines,
-    s_sem, r_sem, ws_sem, wr_sem, bs_sem, br_sem, l_sem,
+    s_sem, r_sem, ws_sem, wr_sem, bs_sem, br_sem, l_sem, i_sem,
 ):
     ngx, ngy, ngz = dims
     nx, ny, nz = g_ref.shape[1:]
@@ -66,6 +66,15 @@
                 )
             awaited = awaited + (count - 1)
 
+    loads = [
+        pltpu.make_async_copy(a, z, i_sem.at[slot])
+        for slot, (a, z) in enumerate(
+            ((g_hbm, g_ref), (w_hbm, w_ref), (d_hbm, d_ref), (b_hbm, b_ref))
+        )
+    ]
+    for load in loads:
+        load.start()
+
     rounds = field.shape[0]
     for name, index, count in axes:
         for side in range(2):
@@ -81,8 +90,6 @@
                         )
                     else:
                         pack_r[r, side] = jnp.zeros(pack_r.shape[2:], jnp.float32)
-
-    pl.semaphore_wait(barrier, awaited)
 
     lane2 = iota((ny, nz), 1)
 
@@ -121,11 +128,15 @@
         if r > 0:
             for e in range(EQ):
                 field[r, e, 0:n] = value[e]
-        for copy, has_target, _, name in made:
-            if name != "gz":
-                @pl.when(has_target)
-                def _():
-                    copy.start()
+        def begin(along_z):
+            for copy, has_target, _, name in made:
+                if (name == "gz") == along_z:
+                    @pl.when(has_target)
+                    def _():
+                        copy.start()
+
+        if r > 0:
+            begin(False)
         low = jnp.zeros((ny, nz), jnp.float32)
         high = jnp.zeros((ny, nz), jnp.float32)
         for e in range(EQ):
@@ -135,11 +146,10 @@
                 high = jnp.where(here, jnp.broadcast_to(value[e][i, :, nz - 1 : nz], (ny, nz)), high)
         pack_s[r, 0] = low
         pack_s[r, 1] = high
-        for copy, has_target, _, name in made:
-            if name == "gz":
-                @pl.when(has_target)
-                def _():
-                    copy.start()
+        if r == 0:
+            pl.semaphore_wait(barrier, awaited)
+            begin(False)
+        begin(True)
 
     def receive(r, n, s):
         for copy, _, has_source, _ in copies(r, n, s):
@@ -276,8 +286,11 @@
         for copy in stage(number, *args):
             copy.wait_recv()
 
+    loads[0].wait()
     v = [g_ref[e] for e in range(EQ)]
     send(0, v, nx, 1)
+    for load in loads[1:]:
+        load.wait()
     for e in range(EQ):
         total = d_ref[e]
         for k in range(6):
@@ -548,10 +561,14 @@
     dma = pltpu.SemaphoreType.DMA
     return pl.pallas_call(
         functools.partial(kernel, dims, cores),
-        out_shape=jax.ShapeDtypeStruct(guess.shape, f32),
-        in_specs=[pl.BlockSpec(memory_space=vmem)] * 4,
+        out_shape=vmem(guess.shape, f32),
+        in_specs=[pl.BlockSpec(memory_space=pl.ANY)] * 4,
         out_specs=pl.BlockSpec(memory_space=vmem),
         scratch_shapes=[
+            vmem(couplings.shape, f32),
+            vmem(diagonal.shape, f32),
+            vmem(right_side.shape, f32),
+            vmem(guess.shape, f32),
             vmem((rounds, EQ) + brick, f32),
             vmem((rounds, 2, EQ, ny, nz), f32),
             vmem((rounds, EQ) + brick, f32),
@@ -576,6 +593,7 @@
             dma,
             dma,
             dma((1,)),
+            dma((4,)),
         ],
         compiler_params=pltpu.CompilerParams(
             collective_id=0, has_side_effects=True, vmem_limit_bytes=60 * 1024 * 1024

time: 39.2 us -> 36.8 us (0.939)
  Pallas kernels: 37.5 us -> 36 us
  local copies, waits for them, and re-layouts: 1.54 us -> 0.64 us
    pallas_call x1, Pallas kernels: 37.5 us -> 36 us  [per_device(): pl.pallas_call(functools.partial(kernel, dims, cores), out_shape=vmem(gue...]
    unnamed x1, local copies, waits for them, and re-layouts: 1.54 us -> 0.64 us
where the time goes in v1:
time: 36.8 us; the launch traced here: 36.7 us
  Pallas kernels  36 us (98%)
  local copies, waits for them, and re-layouts  0.64 us (2%)
    pallas_call x1, Pallas kernels, per_device(): pl.pallas_call(functools.partial(kernel, dims, cores), out_shape=vmem(gue...  36 us

profile of v1, /device:TPU:0, one launch (start us, length us, event | category | flops | bytes accessed | tf_op | source)
XLA Modules:
  0.0 36.7 jit_solution(518348901012212408)
XLA Ops:
  0.0 36.0 %shard_map.46 = f32[3,8,8,128]{3,2,1,0:T(8,128)S(1)} custom-call(f32[18,8,8,128]{3,2,1,0:T(8,128)} %w_hbm.1, f32[3,8,8,128]{3,2,1,0:T(8,128)} %d_hbm.1, f32[3,8,8,128]{3,2,1,0:T(8,128)} %b_hbm.1, f32[3,8,8,128]{3,2,1,0:T(8,128)} %g_hbm.1), custom_call_target="tpu_custom_call" | custom-call | tf_op jit(solution)/shard_map/pallas_call | solution.py:562
  36.0 0.6 %copy.6 = f32[3,8,8,128]{3,2,1,0:T(8,128)} copy(f32[3,8,8,128]{3,2,1,0:T(8,128)S(1)} %shard_map.46) | data formatting | bytes 196608

commit v2 on v1

v2 whole, which is shorter than its diff:
```python
import functools

import jax
import jax.numpy as jnp
from jax import lax
from jax.experimental import pallas as pl
from jax.experimental.pallas import tpu as pltpu
from jax.sharding import PartitionSpec as P

SWEEPS = 2
COARSE_SWEEPS = 8
DAMP = 0.8
KEEP = 1.0 - DAMP
EQ = 3
MESH = pl.DeviceIdType.MESH
HIGH = lax.Precision.HIGHEST
DEEP = (False, True, True, False, True)
FINE = (True, True, False, False, True)


def roll(value, shift, axis):
    size = value.shape[axis]
    shift = shift % size
    return value if shift == 0 else pltpu.roll(value, shift, axis)


def iota(shape, axis):
    return lax.broadcasted_iota(jnp.int32, shape, axis)


class Level:
    def __init__(self, n, s, refs):
        self.n, self.s = n, s
        (self.cw, self.st, self.xw, self.cb, self.tot, self.zs,
         self.xt, self.xst, self.yst, self.yxw, self.zst, self.r_sem) = refs


def kernel(
    dims, cores, w_hbm, d_hbm, b_hbm, g_hbm, out_ref,
    w_ref, d_ref, b_ref, g_ref,
    tally, field, pfield, zpack, hx, hy, hz, px, py, pz, exy, exz, eyz, w1, *rest,
):
    level_refs = (rest[:12], rest[12:24])
    (wsend, wall, bsend, ball, e2, lines,
     s_sem, r_sem, ws_sem, wr_sem, bs_sem, br_sem, l_sem, i_sem, know) = rest[24:]
    ngx, ngy, ngz = dims
    nx, ny, nz = g_ref.shape[1:]
    half = nx // 2
    qx, qy, qz = nx // 4, ny // 4, nz // 4
    rows = ngx * ngy
    nX = ngz // cores
    gx, gy, gz = lax.axis_index("gx"), lax.axis_index("gy"), lax.axis_index("gz")
    X, core = gz // cores, gz % cores
    row = gy * ngx + gx
    axes = (("gx", gx, ngx), ("gy", gy, ngy), ("gz", gz, ngz))
    L0 = Level(nx, 1, level_refs[0])
    L1 = Level(half, 2, level_refs[1])
    tile = (ny, nz)
    yi, zi = iota(tile, 0), iota(tile, 1)
    every = range(EQ)

    def device(**change):
        here = {"gx": gx, "gy": gy, "gz": gz}
        here.update(change)
        return (here["gx"], here["gy"], here["gz"])

    barrier = pltpu.get_barrier_semaphore()
    close = ngy <= 4 and ngz <= 4
    awaited = 0

    def greet(ok, where):
        @pl.when(ok)
        def _():
            pl.semaphore_signal(barrier, inc=1, device_id=where, device_id_type=MESH)
        return ok.astype(jnp.int32)

    for name, index, count in axes:
        if close and name != "gx":
            steps = (-1, 1) if name == "gy" or cores == 1 else (-1, 1, -cores, cores)
            for step in steps:
                ok = (index + step >= 0) & (index + step < count)
                awaited = awaited + greet(ok, device(**{name: jnp.clip(index + step, 0, count - 1)}))
        else:
            for step in range(1, count):
                pl.semaphore_signal(
                    barrier, inc=1, device_id=device(**{name: (index + step) % count}),
                    device_id_type=MESH,
                )
            awaited = awaited + (count - 1)

    loads = [
        pltpu.make_async_copy(a, z, i_sem.at[slot])
        for slot, (a, z) in enumerate(
            ((g_hbm, g_ref), (w_hbm, w_ref), (d_hbm, d_ref), (b_hbm, b_ref))
        )
    ]
    for load in loads:
        load.start()

    there = {
        name: (index > 0, index < count - 1) for name, index, count in axes
    }
    beside = {
        name: (jnp.maximum(index - 1, 0), jnp.minimum(index + 1, count - 1))
        for name, index, count in axes
    }

    def edge_rows(s, lo, hi):
        return (yi < jnp.where(lo, s, 0)) | (yi >= jnp.where(hi, ny - s, ny))

    def remote(a, z, ss, rs, where):
        return pltpu.make_async_remote_copy(
            src_ref=a, dst_ref=z, send_sem=ss, recv_sem=rs,
            device_id=where, device_id_type=MESH,
        )

    def rows_of(side, s):
        return pl.ds(0 if side == 0 else ny - s, s)

    counts = [
        [k for k in (0, 1, 2) if (k > 0 or count == 1) and k < count and (k == 2 or count <= 2 or k == 1)]
        for _, _, count in axes
    ]
    found = [
        there[name][0].astype(jnp.int32) + there[name][1].astype(jnp.int32) for name, _, _ in axes
    ]
    cases = []
    for cx in counts[0]:
        for cy in counts[1]:
            for cz in counts[2]:
                cases.append(((cx, cy, cz), (found[0] == cx) & (found[1] == cy) & (found[2] == cz)))

    def await_rows(sem, number):
        if number > 0:
            part = next(k for k in (8, 4, 2, 1) if number % k == 0)
            ref = tally.at[pl.ds(0, number // part), pl.ds(0, part)]
            pltpu.make_async_copy(ref, ref, sem).wait()

    def await_all(sem, groups):
        for (cx, cy, cz), ok in cases:
            many = {"x": cx, "y": cy, "z": cz, "xy": cx * cy, "xz": cx * cz, "yz": cy * cz}
            number = sum(many[kind] * size for g in groups for kind, size in g.sizes.items())
            if len(cases) == 1:
                await_rows(sem, number)
            else:
                @pl.when(ok)
                def _():
                    await_rows(sem, number)

    class Group:
        def __init__(self, sem):
            self.sem, self.copies, self.sizes = sem, [], {}

        def add(self, kind, side, a, z, where, goes):
            self.copies.append((remote(a, z, s_sem, self.sem, where), goes))
            if side == 0:
                size = 1
                for d in z.shape[:-1]:
                    size *= d
                self.sizes[kind] = self.sizes.get(kind, 0) + size

    def plan(r):
        n, s = (nx, 1) if FINE[r] else (half, 2)
        src = g_ref if r == 0 else field.at[r]
        groups = {k: Group(r_sem.at[r, "vdp".index(k)]) for k in "vdp"}
        kinds = [("v", src, 0, hx, hy, hz)]
        if DEEP[r]:
            kinds.append(("p", pfield.at[r], 1, px, py, pz))
        for side in range(2):
            other = 1 - side
            for group, a, which, zx, zy, zz in kinds:
                g = groups[group]
                g.add("x", side, a.at[:, 0 if side == 0 else n - 1], zx.at[r, other],
                      device(gx=beside["gx"][side]), there["gx"][side])
                g.add("y", side, a.at[:, 0:n, rows_of(side, s)], zy.at[r, :, 0:n, rows_of(other, s)],
                      device(gy=beside["gy"][side]), there["gy"][side])
                g.add("z", side, zpack.at[r, which], zz.at[r, other],
                      device(gz=beside["gz"][side]), there["gz"][side])
        if DEEP[r]:
            g = groups["d"]
            for i in range(2):
                for j in range(2):
                    g.add("xy", 2 * i + j, src.at[:, 0 if i == 0 else n - 1, rows_of(j, s)],
                          exy.at[r, 1 - i, :, rows_of(1 - j, s)],
                          device(gx=beside["gx"][i], gy=beside["gy"][j]),
                          there["gx"][i] & there["gy"][j])
                    g.add("xz", 2 * i + j, zpack.at[r, 0], exz.at[r, 1 - i, 1 - j],
                          device(gx=beside["gx"][i], gz=beside["gz"][j]),
                          there["gx"][i] & there["gz"][j])
                    g.add("yz", 2 * i + j, zpack.at[r, 0, rows_of(i, s)], eyz.at[r, 1 - j, rows_of(1 - i, s)],
                          device(gy=beside["gy"][i], gz=beside["gz"][j]),
                          there["gy"][i] & there["gz"][j])
        return groups

    plans = [plan(r) for r in range(len(DEEP))]

    def plan_constants(L):
        g = Group(L.r_sem)
        for side in range(2):
            other = 1 - side
            x_at, x_ok = device(gx=beside["gx"][side]), there["gx"][side]
            y_at, y_ok = device(gy=beside["gy"][side]), there["gy"][side]
            g.add("x", side, L.xw.at[:, side], L.xt.at[other], x_at, x_ok)
            g.add("x", side, L.st.at[:, :, 0 if side == 0 else L.n - 1], L.xst.at[other], x_at, x_ok)
            g.add("y", side, L.st.at[:, :, :, rows_of(side, L.s)],
                  L.yst.at[:, :, :, rows_of(other, L.s)], y_at, y_ok)
            g.add("y", side, L.xw.at[:, :, rows_of(side, L.s)], L.yxw.at[:, :, rows_of(other, L.s)], y_at, y_ok)
            g.add("z", side, L.zs, L.zst.at[other], device(gz=beside["gz"][side]), there["gz"][side])
        return g

    constants = [plan_constants(L0), plan_constants(L1)]

    def begin(*groups):
        for g in groups:
            for copy, goes in g.copies:
                @pl.when(goes)
                def _():
                    copy.start()

    def arrive(*groups):
        for g in groups:
            await_all(g.sem, [g])

    def pack(L, get, planes=None):
        got = jnp.zeros(tile, jnp.float32)
        for e in every:
            for i in (range(L.n) if planes is None else planes):
                j = e * L.n + i
                got = jnp.where(zi // (2 * L.s) == j, roll(get(e, i), 2 * L.s * j + L.s, 1), got)
        return got

    def unpack(L, tile_of, e, i):
        return roll(tile_of, -(2 * L.s * (e * L.n + i) + L.s), 1)

    def combine(L, low, high, ok=None):
        s = L.s
        up = zi % (2 * s) < s
        has_low, has_high = there["gz"]
        if ok is not None:
            has_low, has_high = has_low & ok, has_high & ok
        code = jnp.where(up, jnp.where(has_high, 1, 0), jnp.where(has_low, 2, 0))
        return jnp.where(code == 1, roll(high, -s, 1), jnp.where(code == 2, roll(low, s, 1), 0.0))

    def local(L, get, e, i):
        n, s = L.n, L.s
        v = get(e, i)
        q = L.cw[e, 2, i] * roll(v, -s, 0) + L.cw[e, 3, i] * roll(v, s, 0)
        q = q + L.cw[e, 4, i] * roll(v, -s, 1) + L.cw[e, 5, i] * roll(v, s, 1)
        if i < n - 1:
            q = q + L.cw[e, 0, i] * get(e, i + 1)
        if i > 0:
            q = q + L.cw[e, 1, i] * get(e, i - 1)
        return q + L.cb[e, i]

    def border(L, q, halo, e, i):
        gx_of, gy_of, gz_of = halo
        q = q + L.st[e, 0, i] * gy_of(e, i) + L.st[e, 1, i] * gz_of(e, i)
        if i == 0:
            q = q + L.xw[e, 0] * gx_of(0, e)
        if i == L.n - 1:
            q = q + L.xw[e, 1] * gx_of(1, e)
        return q

    def received(L, r, x_ref, y_ref, z_ref):
        my = edge_rows(L.s, *there["gy"])
        c = combine(L, z_ref[r, 0], z_ref[r, 1])
        return (
            lambda side, e: jnp.where(there["gx"][side], x_ref[r, side, e], 0.0),
            lambda e, i: jnp.where(my, y_ref[r, e, i], 0.0),
            lambda e, i: unpack(L, c, e, i),
        )

    def ring(L, r, get, own):
        n, s = L.n, L.s
        my = edge_rows(s, *there["gy"])
        lines_of = []
        columns_of = []
        for side in range(2):
            ok = there["gx"][side]
            mask = edge_rows(s, ok & there["gy"][0], ok & there["gy"][1])
            lines_of.append([jnp.where(mask, exy[r, side, e], 0.0) for e in every])
            columns_of.append(combine(L, exz[r, side, 0], exz[r, side, 1], ok))
        cy = jnp.where(my, combine(L, eyz[r, 0], eyz[r, 1]), 0.0)
        rx = [
            [
                jnp.where(
                    there["gx"][side],
                    px[r, side, e] + L.xt[side, e] * get(e, 0 if side == 0 else n - 1)
                    + L.xst[side, e, 0] * lines_of[side][e]
                    + L.xst[side, e, 1] * unpack(L, columns_of[side], e, n - 1 if side == 0 else 0),
                    0.0,
                )
                for e in every
            ]
            for side in range(2)
        ]

        def ry(e, i):
            got = py[r, e, i] + L.yst[e, 0, i] * get(e, i) + L.yst[e, 1, i] * unpack(L, cy, e, i)
            if i == 0:
                got = got + L.yxw[e, 0] * lines_of[0][e]
            if i == n - 1:
                got = got + L.yxw[e, 1] * lines_of[1][e]
            return jnp.where(my, got, 0.0)

        far = 2 * s * (n - 1)
        sideways = jnp.where(
            zi // (2 * s) % n == 0, roll(columns_of[0], -far, 1), roll(columns_of[1], far, 1)
        )
        toward, along_y, along_x = [combine(L, L.zst[0, k], L.zst[1, k]) for k in range(3)]
        c = combine(L, pz[r, 0], pz[r, 1]) + toward * own + along_y * cy + along_x * sideways
        c = jnp.where(zi < 2 * s * EQ * n, c, 0.0)
        return (
            lambda side, e: rx[side][e],
            ry,
            lambda e, i: unpack(L, c, e, i),
        )

    def put(r, L, v):
        for e in every:
            for i in range(L.n):
                field[r, e, i] = v[e][i]

    def planes(f, L):
        return [[f(e, i) for i in range(L.n)] for e in every]

    def deep(r, L):
        get = lambda e, i: field[r, e, i]
        own = pack(L, get)
        zpack[r, 0] = own
        begin(plans[r]["d"], plans[r]["v"])
        for e in every:
            for i in range(L.n):
                pfield[r, e, i] = KEEP * get(e, i) + local(L, get, e, i)
        zpack[r, 1] = pack(L, lambda e, i: pfield[r, e, i])
        begin(plans[r]["p"])

        def finish():
            arrive(plans[r]["v"])
            halo = received(L, r, hx, hy, hz)
            new = planes(lambda e, i: border(L, pfield[r, e, i], halo, e, i), L)

            def outer():
                arrive(plans[r]["d"], plans[r]["p"])
                return ring(L, r, get, zpack[r, 0])

            return new, outer

        return finish

    def coarsen(a, s):
        n = a.shape[0]
        a = jnp.stack([a[2 * i] + a[2 * i + 1] for i in range(n // 2)])
        y, z = iota(a.shape, 1), iota(a.shape, 2)
        a = a + jnp.where((y // s) % 2 == 0, roll(a, -s, 1), roll(a, s, 1))
        a = a + jnp.where((z // s) % 2 == 0, roll(a, -s, 2), roll(a, s, 2))
        return a * 0.125

    source = iota((nz, nz), 0)
    target = iota((nz, nz), 1)
    squeeze = jnp.where(source == 4 * (target % qz), 1.0, 0.0).astype(jnp.float32)

    def to_rows(a):
        m = a.shape[0]
        c = jnp.dot(a.reshape(m * qx * ny, nz), squeeze, precision=HIGH,
                    preferred_element_type=jnp.float32).reshape(m, qx, ny, nz)
        shape = (m, ny, nz)
        lane = iota(shape, 2)
        got = jnp.zeros(shape, jnp.float32)
        for x in range(qx):
            for y in range(qy):
                part = roll(c[:, x], -4 * y, 1)
                got = jnp.where(lane // qz == x * qy + y, part, got)
        return got

    def own(small, whole, sem):
        return pltpu.make_async_copy(
            small.at[:, pl.ds(0, 1)], whole.at[X, core, :, pl.ds(row, 1)], sem
        )

    def stage(number, small, whole, rs):
        made = []
        if number == 0:
            for step in range(1, ngx):
                made.append((small.at[:, pl.ds(0, 1)], whole.at[X, core, :, pl.ds(row, 1)],
                             step, device(gx=(gx + step) % ngx)))
        elif number == 1:
            block = whole.at[X, core, :, pl.ds(gy * ngx, ngx)]
            for step in range(1, ngy):
                made.append((block, block, step, device(gy=(gy + step) % ngy)))
        elif number == 2:
            block = whole.at[X, core]
            for step in range(1, nX):
                made.append((block, block, step, device(gz=((X + step) % nX) * cores + core)))
        else:
            block = whole.at[:, core]
            for step in range(1, cores):
                made.append((block, block, step, device(gz=X * cores + (core + step) % cores)))
        return [
            remote(a, z, ws_sem.at[number], rs.at[number], where)
            for a, z, _, where in made
        ]

    wargs = (wsend, wall, wr_sem)

    def everyone():
        made = []
        for az in range(ngz):
            for ay in range(ngy):
                for ax in range(ngx):
                    if ax + ay + az == 0:
                        continue
                    made.append(remote(
                        bsend.at[:, pl.ds(0, 1)], ball.at[X, core, :, pl.ds(row, 1)],
                        bs_sem, br_sem,
                        ((gx + ax) % ngx, (gy + ay) % ngy, (gz + az) % ngz),
                    ))
        return made

    def start(number):
        for copy in stage(number, *wargs):
            copy.start()

    def stage_rows(number):
        return 7 * EQ * (
            ngx - 1, ngx * (ngy - 1), rows * (nX - 1), nX * rows * (cores - 1)
        )[number]

    def done(number):
        await_rows(wr_sem.at[number], stage_rows(number))

    def scale(L, get_w, get_d, e, i):
        n, s = L.n, L.s
        raw = [get_w(e, k, i) for k in range(6)]
        total = get_d(e, i)
        for k in range(6):
            total = total + raw[k]
        c = DAMP / total
        w = [c * raw[k] for k in range(6)]
        L.tot[e, i] = (1.0 / DAMP) * total
        last_y, first_y, last_z, first_z = yi >= ny - s, yi < s, zi >= nz - s, zi < s
        L.cw[e, 0, i] = w[0]
        L.cw[e, 1, i] = w[1]
        L.cw[e, 2, i] = jnp.where(last_y, 0.0, w[2])
        L.cw[e, 3, i] = jnp.where(first_y, 0.0, w[3])
        L.cw[e, 4, i] = jnp.where(last_z, 0.0, w[4])
        L.cw[e, 5, i] = jnp.where(first_z, 0.0, w[5])
        L.st[e, 0, i] = jnp.where(last_y, w[2], jnp.where(first_y, w[3], 0.0))
        L.st[e, 1, i] = jnp.where(last_z, w[4], jnp.where(first_z, w[5], 0.0))
        if i == 0:
            L.xw[e, 0] = w[1]
        if i == n - 1:
            L.xw[e, 1] = w[0]
        return c

    def pack_constants(L):
        L.zs[0] = pack(L, lambda e, i: L.st[e, 1, i])
        L.zs[1] = pack(L, lambda e, i: L.st[e, 0, i])
        L.zs[2] = pack(L, lambda e, i: L.xw[e, 0 if i == 0 else 1], (0, L.n - 1))

    loads[0].wait()
    guess = lambda e, i: g_ref[e, i]
    zpack[0, 0] = pack(L0, guess)
    pl.semaphore_wait(barrier, awaited)
    begin(plans[0]["v"])
    hear = there["gy"][0].astype(jnp.int32) + there["gy"][1].astype(jnp.int32)

    def tell(k):
        for side in range(2):
            @pl.when(there["gy"][side])
            def _():
                pl.semaphore_signal(
                    know.at[k], inc=1, device_id=device(gy=beside["gy"][side]), device_id_type=MESH
                )

    if close:
        tell(0)
    for load in loads[1:]:
        load.wait()
    for e in every:
        for i in range(nx):
            c = scale(L0, lambda e, k, i: w_ref[6 * e + k, i], lambda e, i: d_ref[e, i], e, i)
            L0.cb[e, i] = c * b_ref[e, i]
    pack_constants(L0)
    begin(constants[0])
    if close:
        pl.semaphore_wait(know.at[0], hear)
        tell(1)
    for e in every:
        for i in range(nx):
            pfield[0, e, i] = KEEP * guess(e, i) + local(L0, guess, e, i)
    for e in every:
        d1 = coarsen(d_ref[e], 1)
        wsend[6 * EQ + e] = to_rows(coarsen(d1, 2)[None])[0]
        for k in range(6):
            w = 0.25 * coarsen(w_ref[6 * e + k], 1)
            w1[6 * e + k] = w
            wsend[6 * e + k] = to_rows((0.25 * coarsen(w, 2))[None])[0]
        for i in range(half):
            c = scale(L1, lambda e, k, i: w1[6 * e + k, i], lambda e, i: d1[i], e, i)
            w1[6 * EQ + e, i] = c
    own(wsend, wall, l_sem).start()
    start(0)
    pack_constants(L1)
    begin(constants[1])

    arrive(plans[0]["v"])
    halo = received(L0, 0, hx, hy, hz)
    put(1, L0, planes(lambda e, i: border(L0, pfield[0, e, i], halo, e, i), L0))
    finish = deep(1, L0)
    own(wsend, wall, l_sem).wait()
    done(0)
    if close:
        pl.semaphore_wait(know.at[1], hear)
    start(1)
    arrive(constants[0])
    v, outer = finish()
    kept0 = field.at[0]
    for e in every:
        for i in range(nx):
            kept0[e, i] = v[e][i]
    get = lambda e, i: kept0[e, i]
    q = planes(lambda e, i: local(L0, get, e, i), L0)
    halo = outer()
    first = []
    for e in every:
        r = jnp.stack([
            L0.tot[e, i] * (border(L0, q[e][i], halo, e, i) - DAMP * get(e, i)) for i in range(nx)
        ])
        b = coarsen(r, 1)
        first.append([])
        for i in range(half):
            u = w1[6 * EQ + e, i] * b[i]
            L1.cb[e, i] = u
            first[e].append(u)
    put(2, L1, first)
    finish = deep(2, L1)
    done(1)
    start(2)
    arrive(constants[1])
    u, outer = finish()
    kept1 = pfield.at[3]
    for e in every:
        for i in range(half):
            kept1[e, i] = u[e][i]
    get = lambda e, i: kept1[e, i]
    q = planes(lambda e, i: local(L1, get, e, i), L1)
    halo = outer()
    rest = []
    for e in every:
        r = jnp.stack([
            L1.tot[e, i] * (border(L1, q[e][i], halo, e, i) - DAMP * get(e, i)) for i in range(half)
        ])
        rest.append(coarsen(r, 2))
    bsend[...] = to_rows(jnp.stack(rest))
    for copy in reversed(everyone()):
        copy.start()
    own(bsend, ball, br_sem).start()
    done(2)
    start(3)
    done(3)

    shape = (ngz, rows, nz)
    r_i, l_i = iota(shape, 1), iota(shape, 2)
    g_i = iota(shape, 0)
    zc, yc, xc = l_i % qz, (l_i // qz) % qy, l_i // (qz * qy)
    gyi, gxi = r_i // ngx, r_i % ngx
    inside = [
        ~((xc == qx - 1) & (gxi == ngx - 1)), ~((xc == 0) & (gxi == 0)),
        ~((yc == qy - 1) & (gyi == ngy - 1)), ~((yc == 0) & (gyi == 0)),
        ~((zc == qz - 1) & (g_i == ngz - 1)), ~((zc == 0) & (g_i == 0)),
    ]

    def whole(ref, index):
        return ref[:, :, index].reshape(shape)

    def next_of(v):
        return jnp.concatenate([v[1:], v[:1]], axis=0)

    def prev_of(v):
        return jnp.concatenate([v[-1:], v[:-1]], axis=0)

    def near2(v):
        sy, sx = qz, qz * qy
        return [
            jnp.where(xc == qx - 1, roll(roll(v, (qx - 1) * sx, 2), -1, 1), roll(v, -sx, 2)),
            jnp.where(xc == 0, roll(roll(v, -(qx - 1) * sx, 2), 1, 1), roll(v, sx, 2)),
            jnp.where(yc == qy - 1, roll(roll(v, (qy - 1) * sy, 2), -ngx, 1), roll(v, -sy, 2)),
            jnp.where(yc == 0, roll(roll(v, -(qy - 1) * sy, 2), ngx, 1), roll(v, sy, 2)),
            jnp.where(zc == qz - 1, roll(next_of(v), qz - 1, 2), roll(v, -1, 2)),
            jnp.where(zc == 0, roll(prev_of(v), -(qz - 1), 2), roll(v, 1, 2)),
        ]

    def dot_near(weights, near):
        total = weights[0] * near[0]
        for k in range(1, 6):
            total = total + weights[k] * near[k]
        return total

    def pair(a):
        sy, sx = qz, qz * qy
        a = a + jnp.where(xc % 2 == 0, roll(a, -sx, 2), roll(a, sx, 2))
        a = a + jnp.where(yc % 2 == 0, roll(a, -sy, 2), roll(a, sy, 2))
        a = a + jnp.where(zc % 2 == 0, roll(a, -1, 2), roll(a, 1, 2))
        return a * 0.125

    groups = qx * qy
    tiles = ngz // groups
    shape3 = (tiles, rows, nz)
    r3, l3, t3 = iota(shape3, 1), iota(shape3, 2), iota(shape3, 0)
    inside3 = [
        r3 % ngx < ngx - 1, r3 % ngx > 0, r3 // ngx < ngy - 1, r3 // ngx > 0,
        ~((l3 >= nz - 2) & (t3 == tiles - 1)), ~((l3 < 2) & (t3 == 0)),
    ]

    def join(a):
        a = a.reshape(tiles, groups, rows, nz)
        got = a[:, 0]
        for j in range(1, groups):
            got = jnp.where(l3 // qz == j, a[:, j], got)
        return got

    def part(a):
        parts = []
        for j in range(groups):
            mine = jnp.where(l3 // qz == j, a, 0.0)
            size = qz
            while size < nz:
                mine = mine + roll(mine, size, 2)
                size *= 2
            parts.append(mine)
        return jnp.stack(parts, axis=1).reshape(shape)

    def near3(v):
        if tiles == 1:
            up, down = roll(v, -2, 2), roll(v, 2, 2)
        else:
            up = jnp.where(l3 >= nz - 2, roll(next_of(v), -2, 2), roll(v, -2, 2))
            down = jnp.where(l3 < 2, roll(prev_of(v), 2, 2), roll(v, 2, 2))
        return [roll(v, -1, 1), roll(v, 1, 1), roll(v, -ngx, 1), roll(v, ngx, 1), up, down]

    w2, t2, w3, t3s = [], [], [], []
    for e in range(EQ):
        plain = [whole(wall, 6 * e + k) for k in range(6)]
        d2 = whole(wall, 6 * EQ + e)
        total = d2
        for k in range(6):
            total = total + plain[k]
        t2.append(total)
        w2.append([jnp.where(inside[k], plain[k], 0.0) for k in range(6)])
        plain3 = [0.25 * join(pair(plain[k])) for k in range(6)]
        total = join(pair(d2))
        for k in range(6):
            total = total + plain3[k]
        t3s.append(total)
        w3.append([jnp.where(inside3[k], plain3[k], 0.0) for k in range(6)])
    c2 = [DAMP / t for t in t2]
    c3 = [DAMP / t for t in t3s]

    pltpu.make_async_copy(ball, ball, br_sem).wait()

    rhs = [whole(ball, e) for e in every]

    def smooth2(v):
        return [KEEP * v[e] + c2[e] * (rhs[e] + dot_near(w2[e], near2(v[e]))) for e in every]

    v2 = [c2[e] * rhs[e] for e in every]
    for step in range(SWEEPS - 1):
        v2 = smooth2(v2)
    rest = [rhs[e] - t2[e] * v2[e] + dot_near(w2[e], near2(v2[e])) for e in every]
    rhs3 = [join(pair(rest[e])) for e in every]
    v3 = [c3[e] * rhs3[e] for e in every]
    for step in range(COARSE_SWEEPS - 1):
        v3 = [KEEP * v3[e] + c3[e] * (rhs3[e] + dot_near(w3[e], near3(v3[e]))) for e in every]
    v2 = [v2[e] + part(v3[e]) for e in every]
    for step in range(SWEEPS):
        v2 = smooth2(v2)
    for e in every:
        e2[e] = v2[e]

    wide = groups * nz
    source = iota((nz, wide), 0)
    target = iota((nz, wide), 1)
    widen = jnp.where(source == (target // nz) * qz + (target % nz) // 4, 1.0, 0.0).astype(jnp.float32)
    around = [(gx, gy, gz, None)]
    for axis, index, count in ((0, gx, ngx), (1, gy, ngy), (2, gz, ngz)):
        for step in (-1, 1):
            at = [gx, gy, gz]
            at[axis] = jnp.clip(index + step, 0, count - 1)
            has = index > 0 if step < 0 else index < count - 1
            around.append((at[0], at[1], at[2], has))
    for e in range(EQ):
        for j, (ax, ay, az, has) in enumerate(around):
            line = e2[e, az, pl.ds(ay * ngx + ax, 1), :]
            if has is not None:
                line = jnp.where(has, line, 0.0)
            lines[e * 7 + j : e * 7 + j + 1, :] = line
    for j in range(EQ * 7, lines.shape[0]):
        lines[j : j + 1, :] = jnp.zeros((1, nz), jnp.float32)
    back = jnp.dot(lines[...], widen, precision=HIGH, preferred_element_type=jnp.float32)
    ysel = iota((ny, nz), 0) // 4

    def strip(e, j, x, y):
        col = (x * qy + y) * nz
        return jnp.broadcast_to(back[e * 7 + j : e * 7 + j + 1, col : col + nz], (ny, nz))

    def plane(e, j, x):
        got = strip(e, j, x, 0)
        for y in range(1, qy):
            got = jnp.where(ysel == y, strip(e, j, x, y), got)
        return got

    left, behind, through = halo

    def add_x(side, e):
        return left(side, e) + plane(e, 1 + side, qx - 1 if side == 0 else 0)

    def add_y(e, i):
        x = i // 2
        return behind(e, i) + jnp.where(
            ysel < qy // 2, strip(e, 3, x, qy - 1), strip(e, 4, x, 0)
        )

    def add_z(e, i):
        x = i // 2
        return through(e, i) + jnp.where(
            zi < nz // 2, roll(plane(e, 5, x), 2, 1), roll(plane(e, 6, x), -2, 1)
        )

    corrected = planes(lambda e, i: kept1[e, i] + plane(e, 0, i // 2), L1)
    get = lambda e, i: corrected[e][i]
    put(3, L1, planes(
        lambda e, i: KEEP * get(e, i) + border(L1, local(L1, get, e, i), (add_x, add_y, add_z), e, i), L1
    ))
    get = lambda e, i: field[3, e, i]
    zpack[3, 0] = pack(L1, get)
    begin(plans[3]["v"])
    q = planes(lambda e, i: KEEP * get(e, i) + local(L1, get, e, i), L1)
    arrive(plans[3]["v"])
    halo = received(L1, 3, hx, hy, hz)
    u = planes(lambda e, i: border(L1, q[e][i], halo, e, i), L1)
    put(4, L0, planes(lambda e, i: kept0[e, i] + u[e][i // 2], L0))
    finish = deep(4, L0)
    v, outer = finish()
    last = pfield.at[0]
    for e in every:
        for i in range(nx):
            last[e, i] = v[e][i]
    get = lambda e, i: last[e, i]
    q = planes(lambda e, i: KEEP * get(e, i) + local(L0, get, e, i), L0)
    halo = outer()
    for e in every:
        for i in range(nx):
            out_ref[e, i] = border(L0, q[e][i], halo, e, i)
    await_all(s_sem, [g for p in plans for g in p.values()] + constants)
    for number in range(4):
        await_rows(ws_sem.at[number], stage_rows(number))
    await_rows(bs_sem, EQ * (rows * ngz - 1))


def per_device(dims, cores, couplings, diagonal, right_side, guess):
    ngx, ngy, ngz = dims
    brick = guess.shape[1:]
    nx, ny, nz = brick
    half = nx // 2
    rows = ngx * ngy
    nX = ngz // cores
    rounds = len(DEEP)
    f32 = jnp.float32
    vmem = pltpu.VMEM
    dma = pltpu.SemaphoreType.DMA

    def level(n):
        return [
            vmem((EQ, 6, n, ny, nz), f32),
            vmem((EQ, 2, n, ny, nz), f32),
            vmem((EQ, 2, ny, nz), f32),
            vmem((EQ, n, ny, nz), f32),
            vmem((EQ, n, ny, nz), f32),
            vmem((3, ny, nz), f32),
            vmem((2, EQ, ny, nz), f32),
            vmem((2, EQ, 2, ny, nz), f32),
            vmem((EQ, 2, n, ny, nz), f32),
            vmem((EQ, 2, ny, nz), f32),
            vmem((2, 3, ny, nz), f32),
            dma,
        ]

    faces = [
        vmem((rounds, 2, EQ, ny, nz), f32),
        vmem((rounds, EQ) + brick, f32),
        vmem((rounds, 2, ny, nz), f32),
    ]
    return pl.pallas_call(
        functools.partial(kernel, dims, cores),
        out_shape=vmem(guess.shape, f32),
        in_specs=[pl.BlockSpec(memory_space=pl.ANY)] * 4,
        out_specs=pl.BlockSpec(memory_space=vmem),
        scratch_shapes=[
            vmem(couplings.shape, f32),
            vmem(diagonal.shape, f32),
            vmem(right_side.shape, f32),
            vmem(guess.shape, f32),
            vmem((max(2048, nX * rows * 7 * EQ * (cores - 1) // 8, rows * (nX - 1) * 7 * EQ // 8), 8, nz), f32),
            vmem((rounds, EQ) + brick, f32),
            vmem((rounds, EQ) + brick, f32),
            vmem((rounds, 2, ny, nz), f32),
            *faces,
            *faces,
            vmem((rounds, 2, EQ, ny, nz), f32),
            vmem((rounds, 2, 2, ny, nz), f32),
            vmem((rounds, 2, ny, nz), f32),
            vmem((7 * EQ, half, ny, nz), f32),
            *level(nx),
            *level(half),
            vmem((7 * EQ, ny, nz), f32),
            vmem((nX, cores, 7 * EQ, rows, nz), f32),
            vmem((EQ, ny, nz), f32),
            vmem((nX, cores, EQ, rows, nz), f32),
            vmem((EQ, ngz, rows, nz), f32),
            vmem((-(-EQ * 7 // 8) * 8, nz), f32),
            dma,
            dma((rounds, 3)),
            dma((4,)),
            dma((4,)),
            dma,
            dma,
            dma,
            dma((4,)),
            pltpu.SemaphoreType.REGULAR((2,)),
        ],
        compiler_params=pltpu.CompilerParams(
            collective_id=0, has_side_effects=True, vmem_limit_bytes=60 * 1024 * 1024
        ),
    )(couplings, diagonal, right_side, guess)


def solution(mesh):
    dims = (mesh.shape["gx"], mesh.shape["gy"], mesh.shape["gz"])
    cores = 2 if dims[2] % 2 == 0 else 1
    spec = P(None, "gx", "gy", "gz")
    return jax.shard_map(
        functools.partial(per_device, dims, cores),
        mesh=mesh,
        in_specs=(spec,) * 4,
        out_specs=spec,
        check_vma=False,
    )
```

time: 36.8 us -> 29.8 us (0.81)
  Pallas kernels: 36 us -> 29 us
    pallas_call x1, Pallas kernels: 36 us -> 29 us  [per_device(): pl.pallas_call(functools.partial(kernel, dims, cores), out_shape=vmem(gue...]
where the time goes in v2:
time: 29.8 us; the launch traced here: 29.6 us
  Pallas kernels  29 us (97%)
  local copies, waits for them, and re-layouts  0.64 us (2%)
    pallas_call x1, Pallas kernels, per_device(): pl.pallas_call(functools.partial(kernel, dims, cores), out_shape=vmem(gue...  29 us
    unnamed x1, local copies, waits for them, and re-layouts  0.64 us

profile of v2, /device:TPU:0, one launch (start us, length us, event | category | flops | bytes accessed | tf_op | source)
XLA Modules:
  0.0 29.6 jit_solution(13233871732485640577)
XLA Ops:
  0.0 29.0 %shard_map.46 = f32[3,8,8,128]{3,2,1,0:T(8,128)S(1)} custom-call(f32[18,8,8,128]{3,2,1,0:T(8,128)} %w_hbm.1, f32[3,8,8,128]{3,2,1,0:T(8,128)} %d_hbm.1, f32[3,8,8,128]{3,2,1,0:T(8,128)} %b_hbm.1, f32[3,8,8,128]{3,2,1,0:T(8,128)} %g_hbm.1), custom_call_target="tpu_custom_call" | custom-call | tf_op jit(solution)/shard_map/pallas_call | solution.py:794
  29.0 0.6 %copy.6 = f32[3,8,8,128]{3,2,1,0:T(8,128)} copy(f32[3,8,8,128]{3,2,1,0:T(8,128)S(1)} %shard_map.46) | data formatting | bytes 196608

commit v3 on v2

--- a/solution.py
+++ b/solution.py
@@ -38,11 +38,11 @@
 def kernel(
     dims, cores, w_hbm, d_hbm, b_hbm, g_hbm, out_ref,
     w_ref, d_ref, b_ref, g_ref,
-    tally, field, pfield, zpack, hx, hy, hz, px, py, pz, exy, exz, eyz, w1, *rest,
+    tally, field, pfield, zpack, hx, hy, hz, px, py, pz, exy, exz, eyz, w1, co, cos, cox, coy, coz, zco, *rest,
 ):
     level_refs = (rest[:12], rest[12:24])
-    (wsend, wall, bsend, ball, e2, lines,
-     s_sem, r_sem, ws_sem, wr_sem, bs_sem, br_sem, l_sem, i_sem, know) = rest[24:]
+    (wsend, wall, bsend, ball, e2, lines, broad, beyond, outside,
+     s_sem, r_sem, co_sem, ws_sem, wr_sem, bs_sem, br_sem, l_sem, i_sem, know) = rest[24:]
     ngx, ngy, ngz = dims
     nx, ny, nz = g_ref.shape[1:]
     half = nx // 2
@@ -208,6 +208,19 @@
             g.add("z", side, L.zs, L.zst.at[other], device(gz=beside["gz"][side]), there["gz"][side])
         return g
 
+    def plan_spreads():
+        g = Group(co_sem)
+        s = L1.s
+        for side in range(2):
+            other = 1 - side
+            g.add("x", side, co.at[:, :, 0 if side == 0 else half - 1], cox.at[other],
+                  device(gx=beside["gx"][side]), there["gx"][side])
+            g.add("y", side, co.at[:, :, :, rows_of(side, s)], coy.at[:, :, :, rows_of(other, s)],
+                  device(gy=beside["gy"][side]), there["gy"][side])
+            g.add("z", side, cos, coz.at[other], device(gz=beside["gz"][side]), there["gz"][side])
+        return g
+
+    spreads = plan_spreads()
     constants = [plan_constants(L0), plan_constants(L1)]
 
     def begin(*groups):
@@ -451,6 +464,15 @@
             L.xw[e, 0] = w[1]
         if i == n - 1:
             L.xw[e, 1] = w[0]
+        if L is L1:
+            odd_y, odd_z = yi // s % 2 == 1, zi // s % 2 == 1
+            co[e, 1, i] = w[0] if i % 2 == 1 else w[1]
+            co[e, 2, i] = jnp.where(odd_y, w[2], w[3])
+            co[e, 3, i] = jnp.where(odd_z, w[4], w[5])
+            co[e, 0, i] = (
+                KEEP + (w[1] if i % 2 == 1 else w[0])
+                + jnp.where(odd_y, w[3], w[2]) + jnp.where(odd_z, w[5], w[4])
+            )
         return c
 
     def pack_constants(L):
@@ -483,9 +505,6 @@
             L0.cb[e, i] = c * b_ref[e, i]
     pack_constants(L0)
     begin(constants[0])
-    if close:
-        pl.semaphore_wait(know.at[0], hear)
-        tell(1)
     for e in every:
         for i in range(nx):
             pfield[0, e, i] = KEEP * guess(e, i) + local(L0, guess, e, i)
@@ -501,13 +520,19 @@
             w1[6 * EQ + e, i] = c
     own(wsend, wall, l_sem).start()
     start(0)
-    pack_constants(L1)
-    begin(constants[1])
+    if close:
+        pl.semaphore_wait(know.at[0], hear)
+        tell(1)
 
     arrive(plans[0]["v"])
     halo = received(L0, 0, hx, hy, hz)
     put(1, L0, planes(lambda e, i: border(L0, pfield[0, e, i], halo, e, i), L0))
     finish = deep(1, L0)
+    pack_constants(L1)
+    begin(constants[1])
+    for m in range(4):
+        cos[m] = pack(L1, lambda e, i: co[e, m, i])
+    begin(spreads)
     own(wsend, wall, l_sem).wait()
     done(0)
     if close:
@@ -548,14 +573,24 @@
     halo = outer()
     rest = []
     for e in every:
-        r = jnp.stack([
-            L1.tot[e, i] * (border(L1, q[e][i], halo, e, i) - DAMP * get(e, i)) for i in range(half)
-        ])
-        rest.append(coarsen(r, 2))
+        r = []
+        for i in range(half):
+            total = border(L1, q[e][i], halo, e, i)
+            field[3, e, i] = KEEP * get(e, i) + total
+            r.append(L1.tot[e, i] * (total - DAMP * get(e, i)))
+        rest.append(coarsen(jnp.stack(r), 2))
     bsend[...] = to_rows(jnp.stack(rest))
     for copy in reversed(everyone()):
         copy.start()
     own(bsend, ball, br_sem).start()
+    zpack[3, 0] = pack(L1, lambda e, i: field[3, e, i])
+    begin(plans[3]["v"])
+    arrive(spreads)
+    for m in range(4):
+        c = combine(L1, coz[0, m], coz[1, m])
+        for e in every:
+            for i in range(half):
+                zco[e, m, i] = unpack(L1, c, e, i)
     done(2)
     start(3)
     done(3)
@@ -592,10 +627,8 @@
         ]
 
     def dot_near(weights, near):
-        total = weights[0] * near[0]
-        for k in range(1, 6):
-            total = total + weights[k] * near[k]
-        return total
+        part = [weights[k] * near[k] for k in range(6)]
+        return ((part[0] + part[1]) + (part[2] + part[3])) + (part[4] + part[5])
 
     def pair(a):
         sy, sx = qz, qz * qy
@@ -639,39 +672,39 @@
             down = jnp.where(l3 < 2, roll(prev_of(v), 2, 2), roll(v, 2, 2))
         return [roll(v, -1, 1), roll(v, 1, 1), roll(v, -ngx, 1), roll(v, ngx, 1), up, down]
 
-    w2, t2, w3, t3s = [], [], [], []
+    w2, t2, w3, c2, c3 = [], [], [], [], []
     for e in range(EQ):
         plain = [whole(wall, 6 * e + k) for k in range(6)]
         d2 = whole(wall, 6 * EQ + e)
         total = d2
         for k in range(6):
             total = total + plain[k]
-        t2.append(total)
-        w2.append([jnp.where(inside[k], plain[k], 0.0) for k in range(6)])
+        t2.append((1.0 / DAMP) * total)
+        c2.append(DAMP / total)
+        w2.append([jnp.where(inside[k], c2[e] * plain[k], 0.0) for k in range(6)])
         plain3 = [0.25 * join(pair(plain[k])) for k in range(6)]
         total = join(pair(d2))
         for k in range(6):
             total = total + plain3[k]
-        t3s.append(total)
-        w3.append([jnp.where(inside3[k], plain3[k], 0.0) for k in range(6)])
-    c2 = [DAMP / t for t in t2]
-    c3 = [DAMP / t for t in t3s]
-
+        c3.append(DAMP / total)
+        w3.append([jnp.where(inside3[k], c3[e] * plain3[k], 0.0) for k in range(6)])
+
+    arrive(plans[3]["v"])
     pltpu.make_async_copy(ball, ball, br_sem).wait()
 
-    rhs = [whole(ball, e) for e in every]
+    rhs = [c2[e] * whole(ball, e) for e in every]
 
     def smooth2(v):
-        return [KEEP * v[e] + c2[e] * (rhs[e] + dot_near(w2[e], near2(v[e]))) for e in every]
-
-    v2 = [c2[e] * rhs[e] for e in every]
+        return [(KEEP * v[e] + rhs[e]) + dot_near(w2[e], near2(v[e])) for e in every]
+
+    v2 = list(rhs)
     for step in range(SWEEPS - 1):
         v2 = smooth2(v2)
-    rest = [rhs[e] - t2[e] * v2[e] + dot_near(w2[e], near2(v2[e])) for e in every]
-    rhs3 = [join(pair(rest[e])) for e in every]
-    v3 = [c3[e] * rhs3[e] for e in every]
+    rest = [t2[e] * ((rhs[e] - DAMP * v2[e]) + dot_near(w2[e], near2(v2[e]))) for e in every]
+    rhs3 = [c3[e] * join(pair(rest[e])) for e in every]
+    v3 = list(rhs3)
     for step in range(COARSE_SWEEPS - 1):
-        v3 = [KEEP * v3[e] + c3[e] * (rhs3[e] + dot_near(w3[e], near3(v3[e]))) for e in every]
+        v3 = [(KEEP * v3[e] + rhs3[e]) + dot_near(w3[e], near3(v3[e])) for e in every]
     v2 = [v2[e] + part(v3[e]) for e in every]
     for step in range(SWEEPS):
         v2 = smooth2(v2)
@@ -682,63 +715,124 @@
     source = iota((nz, wide), 0)
     target = iota((nz, wide), 1)
     widen = jnp.where(source == (target // nz) * qz + (target % nz) // 4, 1.0, 0.0).astype(jnp.float32)
-    around = [(gx, gy, gz, None)]
-    for axis, index, count in ((0, gx, ngx), (1, gy, ngy), (2, gz, ngz)):
-        for step in (-1, 1):
-            at = [gx, gy, gz]
-            at[axis] = jnp.clip(index + step, 0, count - 1)
-            has = index > 0 if step < 0 else index < count - 1
-            around.append((at[0], at[1], at[2], has))
-    for e in range(EQ):
-        for j, (ax, ay, az, has) in enumerate(around):
-            line = e2[e, az, pl.ds(ay * ngx + ax, 1), :]
-            if has is not None:
-                line = jnp.where(has, line, 0.0)
-            lines[e * 7 + j : e * 7 + j + 1, :] = line
-    for j in range(EQ * 7, lines.shape[0]):
-        lines[j : j + 1, :] = jnp.zeros((1, nz), jnp.float32)
-    back = jnp.dot(lines[...], widen, precision=HIGH, preferred_element_type=jnp.float32)
-    ysel = iota((ny, nz), 0) // 4
-
-    def strip(e, j, x, y):
+    here = (gx, gy, gz)
+    names = ("gx", "gy", "gz")
+
+    def line(e, *moves):
+        at, ok = list(here), None
+        for axis, side in moves:
+            at[axis] = beside[names[axis]][side]
+            ok = there[names[axis]][side] if ok is None else ok & there[names[axis]][side]
+        got = e2[e, at[2], pl.ds(at[1] * ngx + at[0], 1), :]
+        return got if ok is None else jnp.where(ok, got, 0.0)
+
+    around = ((), ((0, 0),), ((0, 1),), ((1, 0),), ((1, 1),))
+    for block in range(3):
+        extra = () if block == 0 else ((2, block - 1),)
+        for e in every:
+            for o, moves in enumerate(around):
+                at = 16 * block + 5 * e + o
+                lines[at : at + 1, :] = line(e, *moves, *extra)
+        lines[16 * block + 15 : 16 * block + 16, :] = jnp.zeros((1, nz), jnp.float32)
+    for e in every:
+        for sx in range(2):
+            for sy in range(2):
+                at = 48 + 4 * e + 2 * sx + sy
+                lines[at : at + 1, :] = line(e, (0, sx), (1, sy))
+    lines[60:64, :] = jnp.zeros((4, nz), jnp.float32)
+    broad[...] = jnp.dot(lines[...], widen, precision=HIGH, preferred_element_type=jnp.float32)
+    lane16 = iota((16, nz), 1)
+    for g in range(groups):
+        cols = pl.ds(g * nz, nz)
+        c = broad[0:16, cols]
+        low, high = roll(broad[16:32, cols], 2, 1), roll(broad[32:48, cols], -2, 1)
+        outside[:, cols] = jnp.where(lane16 < nz // 2, low, high)
+        beyond[:, cols] = jnp.where(
+            lane16 < 2, low,
+            jnp.where(lane16 >= nz - 2, high, jnp.where(lane16 % 4 < 2, roll(c, 2, 1), roll(c, -2, 1))),
+        )
+    ysel, yhalf = yi // 4, yi // 2 % 2
+
+    def strip(ref, at, x, y):
         col = (x * qy + y) * nz
-        return jnp.broadcast_to(back[e * 7 + j : e * 7 + j + 1, col : col + nz], (ny, nz))
-
-    def plane(e, j, x):
-        got = strip(e, j, x, 0)
+        return jnp.broadcast_to(ref[at : at + 1, col : col + nz], tile)
+
+    def spot(e, o):
+        return 5 * e + o
+
+    def corner(e, sx, sy):
+        return 48 + 4 * e + 2 * sx + sy
+
+    def plane(ref, at, x):
+        got = strip(ref, at, x, 0)
         for y in range(1, qy):
-            got = jnp.where(ysel == y, strip(e, j, x, y), got)
+            got = jnp.where(ysel == y, strip(ref, at, x, y), got)
         return got
 
-    left, behind, through = halo
+    def across_y(ref, center, minus, plus, x):
+        got = None
+        for y in range(qy):
+            below = strip(ref, center, x, y - 1) if y > 0 else strip(ref, minus, x, qy - 1)
+            above = strip(ref, center, x, y + 1) if y < qy - 1 else strip(ref, plus, x, 0)
+            both = jnp.where(yhalf == 0, below, above)
+            got = both if got is None else jnp.where(ysel == y, both, got)
+        return got
+
+    def across_x(ref, e, i):
+        x = i // 2
+        to = x + 1 if i % 2 == 1 else x - 1
+        if to < 0:
+            return plane(ref, spot(e, 1), qx - 1)
+        return plane(ref, spot(e, 2), 0) if to == qx else plane(ref, spot(e, 0), to)
+
+    def rows_y(ref, e, x):
+        if x < 0:
+            low, high, x = corner(e, 0, 0), corner(e, 0, 1), qx - 1
+        elif x == qx:
+            low, high, x = corner(e, 1, 0), corner(e, 1, 1), 0
+        else:
+            low, high = spot(e, 3), spot(e, 4)
+        return jnp.where(yi < ny // 2, strip(ref, low, x, qy - 1), strip(ref, high, x, 0))
+
+    left, behind, through = received(L1, 3, hx, hy, hz)
+    mine = edge_rows(L1.s, *there["gy"])
 
     def add_x(side, e):
-        return left(side, e) + plane(e, 1 + side, qx - 1 if side == 0 else 0)
+        o, face, near = 1 + side, qx - 1 if side == 0 else 0, 0 if side == 0 else qx - 1
+        got = left(side, e) + cox[side, e, 0] * plane(broad, spot(e, o), face)
+        got = got + cox[side, e, 1] * plane(broad, spot(e, 0), near)
+        got = got + cox[side, e, 2] * across_y(
+            broad, spot(e, o), corner(e, side, 0), corner(e, side, 1), face
+        )
+        got = got + cox[side, e, 3] * plane(beyond, spot(e, o), face)
+        return jnp.where(there["gx"][side], got, 0.0)
 
     def add_y(e, i):
         x = i // 2
-        return behind(e, i) + jnp.where(
-            ysel < qy // 2, strip(e, 3, x, qy - 1), strip(e, 4, x, 0)
-        )
+        got = behind(e, i) + coy[e, 0, i] * rows_y(broad, e, x)
+        got = got + coy[e, 1, i] * rows_y(broad, e, x + 1 if i % 2 == 1 else x - 1)
+        got = got + coy[e, 2, i] * plane(broad, spot(e, 0), x)
+        got = got + coy[e, 3, i] * rows_y(beyond, e, x)
+        return jnp.where(mine, got, 0.0)
 
     def add_z(e, i):
         x = i // 2
-        return through(e, i) + jnp.where(
-            zi < nz // 2, roll(plane(e, 5, x), 2, 1), roll(plane(e, 6, x), -2, 1)
-        )
-
-    corrected = planes(lambda e, i: kept1[e, i] + plane(e, 0, i // 2), L1)
-    get = lambda e, i: corrected[e][i]
-    put(3, L1, planes(
-        lambda e, i: KEEP * get(e, i) + border(L1, local(L1, get, e, i), (add_x, add_y, add_z), e, i), L1
-    ))
-    get = lambda e, i: field[3, e, i]
-    zpack[3, 0] = pack(L1, get)
-    begin(plans[3]["v"])
-    q = planes(lambda e, i: KEEP * get(e, i) + local(L1, get, e, i), L1)
-    arrive(plans[3]["v"])
-    halo = received(L1, 3, hx, hy, hz)
-    u = planes(lambda e, i: border(L1, q[e][i], halo, e, i), L1)
+        got = through(e, i) + zco[e, 0, i] * plane(outside, spot(e, 0), x)
+        got = got + zco[e, 1, i] * across_x(outside, e, i)
+        got = got + zco[e, 2, i] * across_y(outside, spot(e, 0), spot(e, 3), spot(e, 4), x)
+        return got + zco[e, 3, i] * plane(broad, spot(e, 0), x)
+
+    swept = pfield.at[3]
+    for e in every:
+        for i in range(half):
+            x = i // 2
+            got = field[3, e, i] + co[e, 0, i] * plane(broad, spot(e, 0), x)
+            got = got + co[e, 1, i] * across_x(broad, e, i)
+            got = got + co[e, 2, i] * across_y(broad, spot(e, 0), spot(e, 3), spot(e, 4), x)
+            swept[e, i] = got + co[e, 3, i] * plane(beyond, spot(e, 0), x)
+    get = lambda e, i: swept[e, i]
+    halo = (add_x, add_y, add_z)
+    u = planes(lambda e, i: KEEP * get(e, i) + border(L1, local(L1, get, e, i), halo, e, i), L1)
     put(4, L0, planes(lambda e, i: kept0[e, i] + u[e][i // 2], L0))
     finish = deep(4, L0)
     v, outer = finish()
@@ -752,7 +846,7 @@
     for e in every:
         for i in range(nx):
             out_ref[e, i] = border(L0, q[e][i], halo, e, i)
-    await_all(s_sem, [g for p in plans for g in p.values()] + constants)
+    await_all(s_sem, [g for p in plans for g in p.values()] + constants + [spreads])
     for number in range(4):
         await_rows(ws_sem.at[number], stage_rows(number))
     await_rows(bs_sem, EQ * (rows * ngz - 1))
@@ -763,6 +857,7 @@
     brick = guess.shape[1:]
     nx, ny, nz = brick
     half = nx // 2
+    qx, qy = nx // 4, ny // 4
     rows = ngx * ngy
     nX = ngz // cores
     rounds = len(DEEP)
@@ -811,6 +906,12 @@
             vmem((rounds, 2, 2, ny, nz), f32),
             vmem((rounds, 2, ny, nz), f32),
             vmem((7 * EQ, half, ny, nz), f32),
+            vmem((EQ, 4, half, ny, nz), f32),
+            vmem((4, ny, nz), f32),
+            vmem((2, EQ, 4, ny, nz), f32),
+            vmem((EQ, 4, half, ny, nz), f32),
+            vmem((2, 4, ny, nz), f32),
+            vmem((EQ, 4, half, ny, nz), f32),
             *level(nx),
             *level(half),
             vmem((7 * EQ, ny, nz), f32),
@@ -818,9 +919,13 @@
             vmem((EQ, ny, nz), f32),
             vmem((nX, cores, EQ, rows, nz), f32),
             vmem((EQ, ngz, rows, nz), f32),
-            vmem((-(-EQ * 7 // 8) * 8, nz), f32),
+            vmem((64, nz), f32),
+            vmem((64, qx * qy * nz), f32),
+            vmem((16, qx * qy * nz), f32),
+            vmem((16, qx * qy * nz), f32),
             dma,
             dma((rounds, 3)),
+            dma,
             dma((4,)),
             dma((4,)),
             dma,

time: 29.8 us -> 26.7 us (0.90)
  Pallas kernels: 29 us -> 25.9 us
    pallas_call x1, Pallas kernels: 29 us -> 25.9 us  [per_device(): pl.pallas_call(functools.partial(kernel, dims, cores), out_shape=vmem(gue...]
where the time goes in v3:
time: 26.7 us; the launch traced here: 26.5 us
  Pallas kernels  25.9 us (97%)
  local copies, waits for them, and re-layouts  0.64 us (2%)
    pallas_call x1, Pallas kernels, per_device(): pl.pallas_call(functools.partial(kernel, dims, cores), out_shape=vmem(gue...  25.9 us
    unnamed x1, local copies, waits for them, and re-layouts  0.64 us

profile of v3, /device:TPU:0, one launch (start us, length us, event | category | flops | bytes accessed | tf_op | source)
XLA Modules:
  0.0 26.5 jit_solution(4495095933758072412)
XLA Ops:
  0.0 25.9 %shard_map.46 = f32[3,8,8,128]{3,2,1,0:T(8,128)S(1)} custom-call(f32[18,8,8,128]{3,2,1,0:T(8,128)} %w_hbm.1, f32[3,8,8,128]{3,2,1,0:T(8,128)} %d_hbm.1, f32[3,8,8,128]{3,2,1,0:T(8,128)} %b_hbm.1, f32[3,8,8,128]{3,2,1,0:T(8,128)} %g_hbm.1), custom_call_target="tpu_custom_call" | custom-call | tf_op jit(solution)/shard_map/pallas_call | solution.py:889
  25.9 0.6 %copy.6 = f32[3,8,8,128]{3,2,1,0:T(8,128)} copy(f32[3,8,8,128]{3,2,1,0:T(8,128)S(1)} %shard_map.46) | data formatting | bytes 196608

commit v4 on v3

--- a/solution.py
+++ b/solution.py
@@ -41,7 +41,7 @@
     tally, field, pfield, zpack, hx, hy, hz, px, py, pz, exy, exz, eyz, w1, co, cos, cox, coy, coz, zco, *rest,
 ):
     level_refs = (rest[:12], rest[12:24])
-    (wsend, wall, bsend, ball, e2, lines, broad, beyond, outside,
+    (wsend, wall, bsend, ball, e2, lines, broad, widen, mix, mixed,
      s_sem, r_sem, co_sem, ws_sem, wr_sem, bs_sem, br_sem, l_sem, i_sem, know) = rest[24:]
     ngx, ngy, ngz = dims
     nx, ny, nz = g_ref.shape[1:]
@@ -369,21 +369,29 @@
         a = a + jnp.where((z // s) % 2 == 0, roll(a, -s, 2), roll(a, s, 2))
         return a * 0.125
 
+    def select(a, onehot):
+        parts = []
+        for _ in range(3):
+            parts.append(a.astype(jnp.bfloat16))
+            a = a - parts[-1].astype(jnp.float32)
+        got = jnp.dot(jnp.concatenate(parts, axis=0), onehot, preferred_element_type=jnp.float32)
+        m = a.shape[0]
+        return (got[0:m] + got[m : 2 * m]) + got[2 * m :]
+
+    groups = qx * qy
     source = iota((nz, nz), 0)
     target = iota((nz, nz), 1)
-    squeeze = jnp.where(source == 4 * (target % qz), 1.0, 0.0).astype(jnp.float32)
+    squeeze = jnp.where(source == 4 * (target % qz), 1.0, 0.0).astype(jnp.bfloat16)
 
     def to_rows(a):
         m = a.shape[0]
-        c = jnp.dot(a.reshape(m * qx * ny, nz), squeeze, precision=HIGH,
-                    preferred_element_type=jnp.float32).reshape(m, qx, ny, nz)
-        shape = (m, ny, nz)
-        lane = iota(shape, 2)
-        got = jnp.zeros(shape, jnp.float32)
+        c = select(a.reshape(m * qx * ny, nz), squeeze).reshape(m, qx, ny, nz)
+        place = iota((m, ny, nz), 2) // qz
+        got = jnp.zeros((m, ny, nz), jnp.float32)
         for x in range(qx):
             for y in range(qy):
                 part = roll(c[:, x], -4 * y, 1)
-                got = jnp.where(lane // qz == x * qy + y, part, got)
+                got = jnp.where(place == (x * qy + y + gz) % groups, part, got)
         return got
 
     def own(small, whole, sem):
@@ -499,6 +507,20 @@
         tell(0)
     for load in loads[1:]:
         load.wait()
+    level2 = [None] * (7 * EQ)
+    for e in every:
+        d1 = coarsen(d_ref[e], 1)
+        level2[6 * EQ + e] = coarsen(d1, 2)
+        for k in range(6):
+            w = 0.25 * coarsen(w_ref[6 * e + k], 1)
+            w1[6 * e + k] = w
+            level2[6 * e + k] = 0.25 * coarsen(w, 2)
+        for i in range(half):
+            c = scale(L1, lambda e, k, i: w1[6 * e + k, i], lambda e, i: d1[i], e, i)
+            w1[6 * EQ + e, i] = c
+    wsend[...] = to_rows(jnp.stack(level2))
+    own(wsend, wall, l_sem).start()
+    start(0)
     for e in every:
         for i in range(nx):
             c = scale(L0, lambda e, k, i: w_ref[6 * e + k, i], lambda e, i: d_ref[e, i], e, i)
@@ -508,18 +530,6 @@
     for e in every:
         for i in range(nx):
             pfield[0, e, i] = KEEP * guess(e, i) + local(L0, guess, e, i)
-    for e in every:
-        d1 = coarsen(d_ref[e], 1)
-        wsend[6 * EQ + e] = to_rows(coarsen(d1, 2)[None])[0]
-        for k in range(6):
-            w = 0.25 * coarsen(w_ref[6 * e + k], 1)
-            w1[6 * e + k] = w
-            wsend[6 * e + k] = to_rows((0.25 * coarsen(w, 2))[None])[0]
-        for i in range(half):
-            c = scale(L1, lambda e, k, i: w1[6 * e + k, i], lambda e, i: d1[i], e, i)
-            w1[6 * EQ + e, i] = c
-    own(wsend, wall, l_sem).start()
-    start(0)
     if close:
         pl.semaphore_wait(know.at[0], hear)
         tell(1)
@@ -528,17 +538,13 @@
     halo = received(L0, 0, hx, hy, hz)
     put(1, L0, planes(lambda e, i: border(L0, pfield[0, e, i], halo, e, i), L0))
     finish = deep(1, L0)
-    pack_constants(L1)
-    begin(constants[1])
-    for m in range(4):
-        cos[m] = pack(L1, lambda e, i: co[e, m, i])
-    begin(spreads)
     own(wsend, wall, l_sem).wait()
     done(0)
     if close:
         pl.semaphore_wait(know.at[1], hear)
     start(1)
-    arrive(constants[0])
+    pack_constants(L1)
+    begin(constants[1])
     v, outer = finish()
     kept0 = field.at[0]
     for e in every:
@@ -546,6 +552,7 @@
             kept0[e, i] = v[e][i]
     get = lambda e, i: kept0[e, i]
     q = planes(lambda e, i: local(L0, get, e, i), L0)
+    arrive(constants[0])
     halo = outer()
     first = []
     for e in every:
@@ -562,7 +569,9 @@
     finish = deep(2, L1)
     done(1)
     start(2)
-    arrive(constants[1])
+    for m in range(4):
+        cos[m] = pack(L1, lambda e, i: co[e, m, i])
+    begin(spreads)
     u, outer = finish()
     kept1 = pfield.at[3]
     for e in every:
@@ -570,6 +579,7 @@
             kept1[e, i] = u[e][i]
     get = lambda e, i: kept1[e, i]
     q = planes(lambda e, i: local(L1, get, e, i), L1)
+    arrive(constants[1])
     halo = outer()
     rest = []
     for e in every:
@@ -591,245 +601,248 @@
         for e in every:
             for i in range(half):
                 zco[e, m, i] = unpack(L1, c, e, i)
+    NX, NY, NZ = ngx * qx, ngy * qy, ngz * qz
+    shape = (NZ, 3 * nz)
+    kind, t = iota(shape, 1) // nz, iota(shape, 1) % nz
+    base = gz * qz + t // 4
+    wanted = jnp.where(
+        kind == 0, base,
+        jnp.where(
+            kind == 1, base + jnp.where(t % 4 < 2, -1, 1),
+            jnp.where(t < nz // 2, gz * qz - 1, gz * qz + qz),
+        ),
+    )
+    widen[...] = jnp.where(iota(shape, 0) == wanted, 1.0, 0.0).astype(jnp.bfloat16)
+    for e in every:
+        for i in range(NX + 2):
+            if i in (0, NX + 1):
+                e2[e, i] = jnp.zeros((NY + 16, NZ), jnp.float32)
+            else:
+                e2[e, i, 0:8] = jnp.zeros((8, NZ), jnp.float32)
+                e2[e, i, NY + 8 : NY + 16] = jnp.zeros((8, NZ), jnp.float32)
     done(2)
     start(3)
     done(3)
-
-    shape = (ngz, rows, nz)
-    r_i, l_i = iota(shape, 1), iota(shape, 2)
-    g_i = iota(shape, 0)
-    zc, yc, xc = l_i % qz, (l_i // qz) % qy, l_i // (qz * qy)
-    gyi, gxi = r_i // ngx, r_i % ngx
-    inside = [
-        ~((xc == qx - 1) & (gxi == ngx - 1)), ~((xc == 0) & (gxi == 0)),
-        ~((yc == qy - 1) & (gyi == ngy - 1)), ~((yc == 0) & (gyi == 0)),
-        ~((zc == qz - 1) & (g_i == ngz - 1)), ~((zc == 0) & (g_i == 0)),
-    ]
-
-    def whole(ref, index):
-        return ref[:, :, index].reshape(shape)
-
-    def next_of(v):
-        return jnp.concatenate([v[1:], v[:1]], axis=0)
-
-    def prev_of(v):
-        return jnp.concatenate([v[-1:], v[:-1]], axis=0)
-
-    def near2(v):
-        sy, sx = qz, qz * qy
-        return [
-            jnp.where(xc == qx - 1, roll(roll(v, (qx - 1) * sx, 2), -1, 1), roll(v, -sx, 2)),
-            jnp.where(xc == 0, roll(roll(v, -(qx - 1) * sx, 2), 1, 1), roll(v, sx, 2)),
-            jnp.where(yc == qy - 1, roll(roll(v, (qy - 1) * sy, 2), -ngx, 1), roll(v, -sy, 2)),
-            jnp.where(yc == 0, roll(roll(v, -(qy - 1) * sy, 2), ngx, 1), roll(v, sy, 2)),
-            jnp.where(zc == qz - 1, roll(next_of(v), qz - 1, 2), roll(v, -1, 2)),
-            jnp.where(zc == 0, roll(prev_of(v), -(qz - 1), 2), roll(v, 1, 2)),
-        ]
-
-    def dot_near(weights, near):
-        part = [weights[k] * near[k] for k in range(6)]
-        return ((part[0] + part[1]) + (part[2] + part[3])) + (part[4] + part[5])
-
-    def pair(a):
-        sy, sx = qz, qz * qy
-        a = a + jnp.where(xc % 2 == 0, roll(a, -sx, 2), roll(a, sx, 2))
-        a = a + jnp.where(yc % 2 == 0, roll(a, -sy, 2), roll(a, sy, 2))
-        a = a + jnp.where(zc % 2 == 0, roll(a, -1, 2), roll(a, 1, 2))
-        return a * 0.125
-
-    groups = qx * qy
-    tiles = ngz // groups
-    shape3 = (tiles, rows, nz)
-    r3, l3, t3 = iota(shape3, 1), iota(shape3, 2), iota(shape3, 0)
-    inside3 = [
-        r3 % ngx < ngx - 1, r3 % ngx > 0, r3 // ngx < ngy - 1, r3 // ngx > 0,
-        ~((l3 >= nz - 2) & (t3 == tiles - 1)), ~((l3 < 2) & (t3 == 0)),
-    ]
-
-    def join(a):
-        a = a.reshape(tiles, groups, rows, nz)
-        got = a[:, 0]
-        for j in range(1, groups):
-            got = jnp.where(l3 // qz == j, a[:, j], got)
-        return got
-
-    def part(a):
-        parts = []
-        for j in range(groups):
-            mine = jnp.where(l3 // qz == j, a, 0.0)
-            size = qz
-            while size < nz:
-                mine = mine + roll(mine, size, 2)
-                size *= 2
-            parts.append(mine)
-        return jnp.stack(parts, axis=1).reshape(shape)
-
-    def near3(v):
-        if tiles == 1:
-            up, down = roll(v, -2, 2), roll(v, 2, 2)
-        else:
-            up = jnp.where(l3 >= nz - 2, roll(next_of(v), -2, 2), roll(v, -2, 2))
-            down = jnp.where(l3 < 2, roll(prev_of(v), 2, 2), roll(v, 2, 2))
-        return [roll(v, -1, 1), roll(v, 1, 1), roll(v, -ngx, 1), roll(v, ngx, 1), up, down]
-
-    w2, t2, w3, c2, c3 = [], [], [], [], []
-    for e in range(EQ):
-        plain = [whole(wall, 6 * e + k) for k in range(6)]
-        d2 = whole(wall, 6 * EQ + e)
-        total = d2
-        for k in range(6):
-            total = total + plain[k]
-        t2.append((1.0 / DAMP) * total)
-        c2.append(DAMP / total)
-        w2.append([jnp.where(inside[k], c2[e] * plain[k], 0.0) for k in range(6)])
-        plain3 = [0.25 * join(pair(plain[k])) for k in range(6)]
-        total = join(pair(d2))
-        for k in range(6):
-            total = total + plain3[k]
-        c3.append(DAMP / total)
-        w3.append([jnp.where(inside3[k], c3[e] * plain3[k], 0.0) for k in range(6)])
+    def spread(ref, index):
+        place, y_of = iota((rows, nz), 1) // qz, iota((NY, nz), 0) % qy
+        parts = [[] for _ in range(NX)]
+        for t in range(NZ // nz):
+            moved = []
+            for k in range(groups):
+                got = None
+                for p in range(groups):
+                    g = t * groups + (p - k) % groups
+                    a = ref[g // cores, g % cores, index]
+                    got = a if got is None else jnp.where(place == p, a, got)
+                moved.append(roll(got, -k * qz, 1))
+            for x in range(qx):
+                if ngx != qy:
+                    for y in range(qy):
+                        mix[...] = moved[x * qy + y]
+                        for g in range(ngx):
+                            mixed[g, pl.ds(y, ngy, stride=qy), :] = mix[pl.ds(g, ngy, stride=ngx), :]
+                for g in range(ngx):
+                    if ngx != qy:
+                        got = mixed[g]
+                    else:
+                        got = roll(moved[x * qy], -g, 0)
+                        for y in range(1, qy):
+                            got = jnp.where(y_of == y, roll(moved[x * qy + y], y - g, 0), got)
+                    parts[g * qx + x].append(got)
+        return [p[0] if len(p) == 1 else jnp.concatenate(p, axis=1) for p in parts]
+
+    Y, Z = iota((NY, NZ), 0), iota((NY, NZ), 1)
+    even_y, even_z = Y % 2 == 0, Z % 2 == 0
+    pairs = NX // 4
+
+    def halve(a):
+        made = []
+        for p in range(pairs):
+            two = []
+            for x in (2 * p, 2 * p + 1):
+                c = a[2 * x] + a[2 * x + 1]
+                two.append(c + jnp.where(even_y, roll(c, -1, 0), roll(c, 1, 0)))
+            c = jnp.where(even_y, two[0], two[1])
+            made.append(0.125 * (c + jnp.where(even_z, roll(c, -1, 1), roll(c, 1, 1))))
+        return made
+
+    def double(a, x):
+        c = a[x // 4]
+        if x // 2 % 2 == 0:
+            return jnp.where(even_y, c, roll(c, 1, 0))
+        return jnp.where(even_y, roll(c, -1, 0), c)
+
+    def tree(terms):
+        while len(terms) > 1:
+            terms = [
+                terms[k] + terms[k + 1] if k + 1 < len(terms) else terms[k]
+                for k in range(0, len(terms), 2)
+            ]
+        return terms[0]
+
+    def around2(w, v):
+        made = []
+        for x in range(NX):
+            terms = [
+                w[4][x] * roll(v[x], -1, 1), w[5][x] * roll(v[x], 1, 1),
+                w[2][x] * roll(v[x], -1, 0), w[3][x] * roll(v[x], 1, 0),
+            ]
+            if x < NX - 1:
+                terms.append(w[0][x] * v[x + 1])
+            if x > 0:
+                terms.append(w[1][x] * v[x - 1])
+            made.append(tree(terms))
+        return made
+
+    def around3(w, v):
+        made = []
+        for p in range(pairs):
+            up, down = roll(v[p], -1, 0), roll(v[p], 1, 0)
+            if p < pairs - 1:
+                up = jnp.where(even_y, up, roll(v[p + 1], 1, 0))
+            if p > 0:
+                down = jnp.where(even_y, roll(v[p - 1], -1, 0), down)
+            made.append(tree([
+                w[4][p] * roll(v[p], -2, 1), w[5][p] * roll(v[p], 2, 1),
+                w[0][p] * up, w[1][p] * down,
+                w[2][p] * roll(v[p], -2, 0), w[3][p] * roll(v[p], 2, 0),
+            ]))
+        return made
+
+    def inner(w, k, at, last, step):
+        if k == 0 and step == 2:
+            return jnp.where(even_y, w, 0.0) if at == last else w
+        if k == 1 and step == 2:
+            return jnp.where(even_y, 0.0, w) if at == 0 else w
+        if k < 2:
+            return w
+        return jnp.where((Y >= NY - step, Y < step, Z >= NZ - step, Z < step)[k - 2], 0.0, w)
+
+    def constants_of(plain, diagonal, count, step):
+        scaled, totals, weights = [], [], [[] for _ in range(6)]
+        for at in range(count):
+            total = diagonal[at] + tree([plain[k][at] for k in range(6)])
+            scaled.append(DAMP / total)
+            totals.append((1.0 / DAMP) * total)
+            for k in range(6):
+                weights[k].append(inner(scaled[at] * plain[k][at], k, at, count - 1, step))
+        return scaled, totals, weights
+
+    c2, t2, w2, c3, w3 = [], [], [], [], []
+    for e in every:
+        plain = [spread(wall, 6 * e + k) for k in range(6)]
+        diagonal = spread(wall, 6 * EQ + e)
+        scaled, totals, weights = constants_of(plain, diagonal, NX, 1)
+        c2.append(scaled)
+        t2.append(totals)
+        w2.append(weights)
+        coarse = [[0.25 * c for c in halve(plain[k])] for k in range(6)]
+        scaled, _, weights = constants_of(coarse, halve(diagonal), pairs, 2)
+        c3.append(scaled)
+        w3.append(weights)
 
     arrive(plans[3]["v"])
     pltpu.make_async_copy(ball, ball, br_sem).wait()
-
-    rhs = [c2[e] * whole(ball, e) for e in every]
+    rhs = []
+    for e in every:
+        got = spread(ball, e)
+        rhs.append([c2[e][x] * got[x] for x in range(NX)])
 
     def smooth2(v):
-        return [(KEEP * v[e] + rhs[e]) + dot_near(w2[e], near2(v[e])) for e in every]
-
-    v2 = list(rhs)
+        made = []
+        for e in every:
+            sums = around2(w2[e], v[e])
+            made.append([(KEEP * v[e][x] + rhs[e][x]) + sums[x] for x in range(NX)])
+        return made
+
+    v2 = rhs
     for step in range(SWEEPS - 1):
         v2 = smooth2(v2)
-    rest = [t2[e] * ((rhs[e] - DAMP * v2[e]) + dot_near(w2[e], near2(v2[e]))) for e in every]
-    rhs3 = [c3[e] * join(pair(rest[e])) for e in every]
-    v3 = list(rhs3)
+    rhs3 = []
+    for e in every:
+        sums = around2(w2[e], v2[e])
+        got = halve([t2[e][x] * ((rhs[e][x] - DAMP * v2[e][x]) + sums[x]) for x in range(NX)])
+        rhs3.append([c3[e][p] * got[p] for p in range(pairs)])
+    v3 = rhs3
     for step in range(COARSE_SWEEPS - 1):
-        v3 = [(KEEP * v3[e] + rhs3[e]) + dot_near(w3[e], near3(v3[e])) for e in every]
-    v2 = [v2[e] + part(v3[e]) for e in every]
+        sums = [around3(w3[e], v3[e]) for e in every]
+        v3 = [
+            [(KEEP * v3[e][p] + rhs3[e][p]) + sums[e][p] for p in range(pairs)] for e in every
+        ]
+    v2 = [[v2[e][x] + double(v3[e], x) for x in range(NX)] for e in every]
     for step in range(SWEEPS):
         v2 = smooth2(v2)
     for e in every:
-        e2[e] = v2[e]
-
-    wide = groups * nz
-    source = iota((nz, wide), 0)
-    target = iota((nz, wide), 1)
-    widen = jnp.where(source == (target // nz) * qz + (target % nz) // 4, 1.0, 0.0).astype(jnp.float32)
-    here = (gx, gy, gz)
-    names = ("gx", "gy", "gz")
-
-    def line(e, *moves):
-        at, ok = list(here), None
-        for axis, side in moves:
-            at[axis] = beside[names[axis]][side]
-            ok = there[names[axis]][side] if ok is None else ok & there[names[axis]][side]
-        got = e2[e, at[2], pl.ds(at[1] * ngx + at[0], 1), :]
-        return got if ok is None else jnp.where(ok, got, 0.0)
-
-    around = ((), ((0, 0),), ((0, 1),), ((1, 0),), ((1, 1),))
-    for block in range(3):
-        extra = () if block == 0 else ((2, block - 1),)
-        for e in every:
-            for o, moves in enumerate(around):
-                at = 16 * block + 5 * e + o
-                lines[at : at + 1, :] = line(e, *moves, *extra)
-        lines[16 * block + 15 : 16 * block + 16, :] = jnp.zeros((1, nz), jnp.float32)
-    for e in every:
-        for sx in range(2):
-            for sy in range(2):
-                at = 48 + 4 * e + 2 * sx + sy
-                lines[at : at + 1, :] = line(e, (0, sx), (1, sy))
-    lines[60:64, :] = jnp.zeros((4, nz), jnp.float32)
-    broad[...] = jnp.dot(lines[...], widen, precision=HIGH, preferred_element_type=jnp.float32)
-    lane16 = iota((16, nz), 1)
-    for g in range(groups):
-        cols = pl.ds(g * nz, nz)
-        c = broad[0:16, cols]
-        low, high = roll(broad[16:32, cols], 2, 1), roll(broad[32:48, cols], -2, 1)
-        outside[:, cols] = jnp.where(lane16 < nz // 2, low, high)
-        beyond[:, cols] = jnp.where(
-            lane16 < 2, low,
-            jnp.where(lane16 >= nz - 2, high, jnp.where(lane16 % 4 < 2, roll(c, 2, 1), roll(c, -2, 1))),
-        )
+        for x in range(NX):
+            e2[e, x + 1, 8 : 8 + NY] = v2[e][x]
+
+    wx, wy = qx + 2, qy + 2
+    for e in every:
+        for i in range(wx):
+            for j in range(wy):
+                at = (e * wx + i) * wy + j
+                lines[at : at + 1, :] = e2[e, gx * qx + i, pl.ds(7 + gy * qy + j, 1), :]
+    broad[...] = select(lines[...], widen[...])
+    CENTER, BEYOND_Z, OUTSIDE_Z = range(3)
     ysel, yhalf = yi // 4, yi // 2 % 2
 
-    def strip(ref, at, x, y):
-        col = (x * qy + y) * nz
-        return jnp.broadcast_to(ref[at : at + 1, col : col + nz], tile)
-
-    def spot(e, o):
-        return 5 * e + o
-
-    def corner(e, sx, sy):
-        return 48 + 4 * e + 2 * sx + sy
-
-    def plane(ref, at, x):
-        got = strip(ref, at, x, 0)
+    def strip(kind, e, x, y):
+        at = (e * wx + x + 1) * wy + y + 1
+        return jnp.broadcast_to(broad[at : at + 1, kind * nz : kind * nz + nz], tile)
+
+    def plane(kind, e, x):
+        got = strip(kind, e, x, 0)
         for y in range(1, qy):
-            got = jnp.where(ysel == y, strip(ref, at, x, y), got)
+            got = jnp.where(ysel == y, strip(kind, e, x, y), got)
         return got
 
-    def across_y(ref, center, minus, plus, x):
+    def across_y(kind, e, x):
         got = None
         for y in range(qy):
-            below = strip(ref, center, x, y - 1) if y > 0 else strip(ref, minus, x, qy - 1)
-            above = strip(ref, center, x, y + 1) if y < qy - 1 else strip(ref, plus, x, 0)
-            both = jnp.where(yhalf == 0, below, above)
+            both = jnp.where(yhalf == 0, strip(kind, e, x, y - 1), strip(kind, e, x, y + 1))
             got = both if got is None else jnp.where(ysel == y, both, got)
         return got
 
-    def across_x(ref, e, i):
-        x = i // 2
-        to = x + 1 if i % 2 == 1 else x - 1
-        if to < 0:
-            return plane(ref, spot(e, 1), qx - 1)
-        return plane(ref, spot(e, 2), 0) if to == qx else plane(ref, spot(e, 0), to)
-
-    def rows_y(ref, e, x):
-        if x < 0:
-            low, high, x = corner(e, 0, 0), corner(e, 0, 1), qx - 1
-        elif x == qx:
-            low, high, x = corner(e, 1, 0), corner(e, 1, 1), 0
-        else:
-            low, high = spot(e, 3), spot(e, 4)
-        return jnp.where(yi < ny // 2, strip(ref, low, x, qy - 1), strip(ref, high, x, 0))
+    def across_x(kind, e, i):
+        return plane(kind, e, i // 2 + (1 if i % 2 == 1 else -1))
+
+    def rows_y(kind, e, x):
+        return jnp.where(yi < ny // 2, strip(kind, e, x, -1), strip(kind, e, x, qy))
 
     left, behind, through = received(L1, 3, hx, hy, hz)
     mine = edge_rows(L1.s, *there["gy"])
 
     def add_x(side, e):
-        o, face, near = 1 + side, qx - 1 if side == 0 else 0, 0 if side == 0 else qx - 1
-        got = left(side, e) + cox[side, e, 0] * plane(broad, spot(e, o), face)
-        got = got + cox[side, e, 1] * plane(broad, spot(e, 0), near)
-        got = got + cox[side, e, 2] * across_y(
-            broad, spot(e, o), corner(e, side, 0), corner(e, side, 1), face
-        )
-        got = got + cox[side, e, 3] * plane(beyond, spot(e, o), face)
+        face, near = (-1, 0) if side == 0 else (qx, qx - 1)
+        got = left(side, e) + cox[side, e, 0] * plane(CENTER, e, face)
+        got = got + cox[side, e, 1] * plane(CENTER, e, near)
+        got = got + cox[side, e, 2] * across_y(CENTER, e, face)
+        got = got + cox[side, e, 3] * plane(BEYOND_Z, e, face)
         return jnp.where(there["gx"][side], got, 0.0)
 
     def add_y(e, i):
         x = i // 2
-        got = behind(e, i) + coy[e, 0, i] * rows_y(broad, e, x)
-        got = got + coy[e, 1, i] * rows_y(broad, e, x + 1 if i % 2 == 1 else x - 1)
-        got = got + coy[e, 2, i] * plane(broad, spot(e, 0), x)
-        got = got + coy[e, 3, i] * rows_y(beyond, e, x)
+        got = behind(e, i) + coy[e, 0, i] * rows_y(CENTER, e, x)
+        got = got + coy[e, 1, i] * rows_y(CENTER, e, x + 1 if i % 2 == 1 else x - 1)
+        got = got + coy[e, 2, i] * plane(CENTER, e, x)
+        got = got + coy[e, 3, i] * rows_y(BEYOND_Z, e, x)
         return jnp.where(mine, got, 0.0)
 
     def add_z(e, i):
         x = i // 2
-        got = through(e, i) + zco[e, 0, i] * plane(outside, spot(e, 0), x)
-        got = got + zco[e, 1, i] * across_x(outside, e, i)
-        got = got + zco[e, 2, i] * across_y(outside, spot(e, 0), spot(e, 3), spot(e, 4), x)
-        return got + zco[e, 3, i] * plane(broad, spot(e, 0), x)
+        got = through(e, i) + zco[e, 0, i] * plane(OUTSIDE_Z, e, x)
+        got = got + zco[e, 1, i] * across_x(OUTSIDE_Z, e, i)
+        got = got + zco[e, 2, i] * across_y(OUTSIDE_Z, e, x)
+        return got + zco[e, 3, i] * plane(CENTER, e, x)
 
     swept = pfield.at[3]
     for e in every:
         for i in range(half):
             x = i // 2
-            got = field[3, e, i] + co[e, 0, i] * plane(broad, spot(e, 0), x)
-            got = got + co[e, 1, i] * across_x(broad, e, i)
-            got = got + co[e, 2, i] * across_y(broad, spot(e, 0), spot(e, 3), spot(e, 4), x)
-            swept[e, i] = got + co[e, 3, i] * plane(beyond, spot(e, 0), x)
+            got = field[3, e, i] + co[e, 0, i] * plane(CENTER, e, x)
+            got = got + co[e, 1, i] * across_x(CENTER, e, i)
+            got = got + co[e, 2, i] * across_y(CENTER, e, x)
+            swept[e, i] = got + co[e, 3, i] * plane(BEYOND_Z, e, x)
     get = lambda e, i: swept[e, i]
     halo = (add_x, add_y, add_z)
     u = planes(lambda e, i: KEEP * get(e, i) + border(L1, local(L1, get, e, i), halo, e, i), L1)
@@ -857,7 +870,7 @@
     brick = guess.shape[1:]
     nx, ny, nz = brick
     half = nx // 2
-    qx, qy = nx // 4, ny // 4
+    qx, qy, qz = nx // 4, ny // 4, nz // 4
     rows = ngx * ngy
     nX = ngz // cores
     rounds = len(DEEP)
@@ -918,11 +931,12 @@
             vmem((nX, cores, 7 * EQ, rows, nz), f32),
             vmem((EQ, ny, nz), f32),
             vmem((nX, cores, EQ, rows, nz), f32),
-            vmem((EQ, ngz, rows, nz), f32),
-            vmem((64, nz), f32),
-            vmem((64, qx * qy * nz), f32),
-            vmem((16, qx * qy * nz), f32),
-            vmem((16, qx * qy * nz), f32),
+            vmem((EQ, ngx * qx + 2, ngy * qy + 16, ngz * qz), f32),
+            vmem((EQ * (qx + 2) * (qy + 2), ngz * qz), f32),
+            vmem((EQ * (qx + 2) * (qy + 2), 3 * nz), f32),
+            vmem((ngz * qz, 3 * nz), jnp.bfloat16),
+            vmem((rows, nz), f32),
+            vmem((ngx, ngy * qy, nz), f32),
             dma,
             dma((rounds, 3)),
             dma,

time: 26.7 us -> 25.8 us (0.966)
  Pallas kernels: 25.9 us -> 25 us
    pallas_call x1, Pallas kernels: 25.9 us -> 25 us  [per_device(): pl.pallas_call(functools.partial(kernel, dims, cores), out_shape=vmem(gue...]
where the time goes in v4:
time: 25.8 us; the launch traced here: 25.6 us
  Pallas kernels  25 us (97%)
  local copies, waits for them, and re-layouts  0.64 us (2%)
    pallas_call x1, Pallas kernels, per_device(): pl.pallas_call(functools.partial(kernel, dims, cores), out_shape=vmem(gue...  25 us
    unnamed x1, local copies, waits for them, and re-layouts  0.64 us

profile of v4, /device:TPU:0, one launch (start us, length us, event | category | flops | bytes accessed | tf_op | source)
XLA Modules:
  0.0 25.6 jit_solution(8333663063467584997)
XLA Ops:
  0.0 25.0 %shard_map.46 = f32[3,8,8,128]{3,2,1,0:T(8,128)S(1)} custom-call(f32[18,8,8,128]{3,2,1,0:T(8,128)} %w_hbm.1, f32[3,8,8,128]{3,2,1,0:T(8,128)} %d_hbm.1, f32[3,8,8,128]{3,2,1,0:T(8,128)} %b_hbm.1, f32[3,8,8,128]{3,2,1,0:T(8,128)} %g_hbm.1), custom_call_target="tpu_custom_call" | custom-call | tf_op jit(solution)/shard_map/pallas_call | solution.py:902
  25.0 0.6 %copy.6 = f32[3,8,8,128]{3,2,1,0:T(8,128)} copy(f32[3,8,8,128]{3,2,1,0:T(8,128)S(1)} %shard_map.46) | data formatting | bytes 196608

commit v5 on v4

--- a/solution.py
+++ b/solution.py
@@ -32,7 +32,7 @@
     def __init__(self, n, s, refs):
         self.n, self.s = n, s
         (self.cw, self.st, self.xw, self.cb, self.tot, self.zs,
-         self.xt, self.xst, self.yst, self.yxw, self.zst, self.r_sem) = refs
+         self.xt, self.xst, self.yst, self.yzs, self.yxw, self.zst, self.r_sem) = refs
 
 
 def kernel(
@@ -40,9 +40,9 @@
     w_ref, d_ref, b_ref, g_ref,
     tally, field, pfield, zpack, hx, hy, hz, px, py, pz, exy, exz, eyz, w1, co, cos, cox, coy, coz, zco, *rest,
 ):
-    level_refs = (rest[:12], rest[12:24])
+    level_refs = (rest[:13], rest[13:26])
     (wsend, wall, bsend, ball, e2, lines, broad, widen, mix, mixed,
-     s_sem, r_sem, co_sem, ws_sem, wr_sem, bs_sem, br_sem, l_sem, i_sem, know) = rest[24:]
+     s_sem, r_sem, co_sem, ws_sem, wr_sem, bs_sem, br_sem, i_sem, know) = rest[26:]
     ngx, ngy, ngz = dims
     nx, ny, nz = g_ref.shape[1:]
     half = nx // 2
@@ -64,6 +64,8 @@
         here.update(change)
         return (here["gx"], here["gy"], here["gz"])
 
+    guess_load = pltpu.make_async_copy(g_hbm, g_ref, i_sem.at[0])
+    guess_load.start()
     barrier = pltpu.get_barrier_semaphore()
     close = ngy <= 4 and ngz <= 4
     awaited = 0
@@ -88,14 +90,8 @@
                 )
             awaited = awaited + (count - 1)
 
-    loads = [
-        pltpu.make_async_copy(a, z, i_sem.at[slot])
-        for slot, (a, z) in enumerate(
-            ((g_hbm, g_ref), (w_hbm, w_ref), (d_hbm, d_ref), (b_hbm, b_ref))
-        )
-    ]
-    for load in loads:
-        load.start()
+    for a, z in ((w_hbm, w_ref), (d_hbm, d_ref), (b_hbm, b_ref)):
+        pltpu.make_async_copy(a, z, i_sem.at[1]).start()
 
     there = {
         name: (index > 0, index < count - 1) for name, index, count in axes
@@ -152,41 +148,53 @@
             self.sem, self.copies, self.sizes = sem, [], {}
 
         def add(self, kind, side, a, z, where, goes):
-            self.copies.append((remote(a, z, s_sem, self.sem, where), goes))
+            self.copies.append((kind, remote(a, z, s_sem, self.sem, where), goes))
             if side == 0:
                 size = 1
                 for d in z.shape[:-1]:
                     size *= d
                 self.sizes[kind] = self.sizes.get(kind, 0) + size
 
+    def sides_of_x(n):
+        if ngx == 2:
+            return [(0, (1 - gx) * (n - 1), 1 - gx, gx, 1 - gx, True)]
+        return [
+            (side, 0 if side == 0 else n - 1, side, 1 - side, beside["gx"][side], there["gx"][side])
+            for side in range(2)
+        ]
+
+    def both(a, b):
+        return b if a is True else a & b
+
     def plan(r):
         n, s = (nx, 1) if FINE[r] else (half, 2)
         src = g_ref if r == 0 else field.at[r]
-        groups = {k: Group(r_sem.at[r, "vdp".index(k)]) for k in "vdp"}
+        groups = {k: Group(r_sem.at[r % 2 if k == "v" else 2 + r // 2 % 2]) for k in "vdp"}
         kinds = [("v", src, 0, hx, hy, hz)]
         if DEEP[r]:
             kinds.append(("p", pfield.at[r], 1, px, py, pz))
+        for side, plane_at, _, other, to, ok in sides_of_x(n):
+            for group, a, which, zx, zy, zz in kinds:
+                groups[group].add("x", side, a.at[:, plane_at], zx.at[r, other], device(gx=to), ok)
         for side in range(2):
             other = 1 - side
             for group, a, which, zx, zy, zz in kinds:
                 g = groups[group]
-                g.add("x", side, a.at[:, 0 if side == 0 else n - 1], zx.at[r, other],
-                      device(gx=beside["gx"][side]), there["gx"][side])
                 g.add("y", side, a.at[:, 0:n, rows_of(side, s)], zy.at[r, :, 0:n, rows_of(other, s)],
                       device(gy=beside["gy"][side]), there["gy"][side])
                 g.add("z", side, zpack.at[r, which], zz.at[r, other],
                       device(gz=beside["gz"][side]), there["gz"][side])
         if DEEP[r]:
             g = groups["d"]
+            for i, plane_at, _, other, to, ok in sides_of_x(n):
+                for j in range(2):
+                    g.add("xy", 2 * i + j, src.at[:, plane_at, rows_of(j, s)],
+                          exy.at[r, other, :, rows_of(1 - j, s)],
+                          device(gx=to, gy=beside["gy"][j]), both(ok, there["gy"][j]))
+                    g.add("xz", 2 * i + j, zpack.at[r, 0], exz.at[r, other, 1 - j],
+                          device(gx=to, gz=beside["gz"][j]), both(ok, there["gz"][j]))
             for i in range(2):
                 for j in range(2):
-                    g.add("xy", 2 * i + j, src.at[:, 0 if i == 0 else n - 1, rows_of(j, s)],
-                          exy.at[r, 1 - i, :, rows_of(1 - j, s)],
-                          device(gx=beside["gx"][i], gy=beside["gy"][j]),
-                          there["gx"][i] & there["gy"][j])
-                    g.add("xz", 2 * i + j, zpack.at[r, 0], exz.at[r, 1 - i, 1 - j],
-                          device(gx=beside["gx"][i], gz=beside["gz"][j]),
-                          there["gx"][i] & there["gz"][j])
                     g.add("yz", 2 * i + j, zpack.at[r, 0, rows_of(i, s)], eyz.at[r, 1 - j, rows_of(1 - i, s)],
                           device(gy=beside["gy"][i], gz=beside["gz"][j]),
                           there["gy"][i] & there["gz"][j])
@@ -196,14 +204,15 @@
 
     def plan_constants(L):
         g = Group(L.r_sem)
+        for side, plane_at, mine, other, to, ok in sides_of_x(L.n):
+            g.add("x", side, L.xw.at[:, mine], L.xt.at[other], device(gx=to), ok)
+            g.add("x", side, L.st.at[:, :, plane_at], L.xst.at[other], device(gx=to), ok)
         for side in range(2):
             other = 1 - side
-            x_at, x_ok = device(gx=beside["gx"][side]), there["gx"][side]
             y_at, y_ok = device(gy=beside["gy"][side]), there["gy"][side]
-            g.add("x", side, L.xw.at[:, side], L.xt.at[other], x_at, x_ok)
-            g.add("x", side, L.st.at[:, :, 0 if side == 0 else L.n - 1], L.xst.at[other], x_at, x_ok)
-            g.add("y", side, L.st.at[:, :, :, rows_of(side, L.s)],
-                  L.yst.at[:, :, :, rows_of(other, L.s)], y_at, y_ok)
+            g.add("y", side, L.st.at[:, 0, :, rows_of(side, L.s)],
+                  L.yst.at[:, :, rows_of(other, L.s)], y_at, y_ok)
+            g.add("y", side, L.zs.at[0, rows_of(side, L.s)], L.yzs.at[rows_of(other, L.s)], y_at, y_ok)
             g.add("y", side, L.xw.at[:, :, rows_of(side, L.s)], L.yxw.at[:, :, rows_of(other, L.s)], y_at, y_ok)
             g.add("z", side, L.zs, L.zst.at[other], device(gz=beside["gz"][side]), there["gz"][side])
         return g
@@ -211,10 +220,10 @@
     def plan_spreads():
         g = Group(co_sem)
         s = L1.s
+        for side, plane_at, _, other, to, ok in sides_of_x(half):
+            g.add("x", side, co.at[:, :, plane_at], cox.at[other], device(gx=to), ok)
         for side in range(2):
             other = 1 - side
-            g.add("x", side, co.at[:, :, 0 if side == 0 else half - 1], cox.at[other],
-                  device(gx=beside["gx"][side]), there["gx"][side])
             g.add("y", side, co.at[:, :, :, rows_of(side, s)], coy.at[:, :, :, rows_of(other, s)],
                   device(gy=beside["gy"][side]), there["gy"][side])
             g.add("z", side, cos, coz.at[other], device(gz=beside["gz"][side]), there["gz"][side])
@@ -223,16 +232,21 @@
     spreads = plan_spreads()
     constants = [plan_constants(L0), plan_constants(L1)]
 
-    def begin(*groups):
+    def begin(*groups, only=None):
         for g in groups:
-            for copy, goes in g.copies:
+            for kind, copy, goes in g.copies:
+                if only is not None and kind not in only:
+                    continue
+                if goes is True:
+                    copy.start()
+                    continue
+
                 @pl.when(goes)
                 def _():
                     copy.start()
 
     def arrive(*groups):
-        for g in groups:
-            await_all(g.sem, [g])
+        await_all(groups[0].sem, groups)
 
     def pack(L, get, planes=None):
         got = jnp.zeros(tile, jnp.float32)
@@ -266,13 +280,17 @@
         return q + L.cb[e, i]
 
     def border(L, q, halo, e, i):
-        gx_of, gy_of, gz_of = halo
-        q = q + L.st[e, 0, i] * gy_of(e, i) + L.st[e, 1, i] * gz_of(e, i)
+        gx_of, gy_of, term_z = halo
+        q = q + L.st[e, 0, i] * gy_of(e, i) + term_z(e, i)
         if i == 0:
             q = q + L.xw[e, 0] * gx_of(0, e)
         if i == L.n - 1:
             q = q + L.xw[e, 1] * gx_of(1, e)
         return q
+
+    def ends(L, packed):
+        at = (zi < L.s) | (zi >= nz - L.s)
+        return lambda e, i: jnp.where(at, unpack(L, packed, e, i), 0.0)
 
     def received(L, r, x_ref, y_ref, z_ref):
         my = edge_rows(L.s, *there["gy"])
@@ -280,7 +298,8 @@
         return (
             lambda side, e: jnp.where(there["gx"][side], x_ref[r, side, e], 0.0),
             lambda e, i: jnp.where(my, y_ref[r, e, i], 0.0),
-            lambda e, i: unpack(L, c, e, i),
+            ends(L, L.zs[0] * c),
+            c,
         )
 
     def ring(L, r, get, own):
@@ -309,7 +328,7 @@
         ]
 
         def ry(e, i):
-            got = py[r, e, i] + L.yst[e, 0, i] * get(e, i) + L.yst[e, 1, i] * unpack(L, cy, e, i)
+            got = py[r, e, i] + L.yst[e, i] * get(e, i)
             if i == 0:
                 got = got + L.yxw[e, 0] * lines_of[0][e]
             if i == n - 1:
@@ -323,10 +342,11 @@
         toward, along_y, along_x = [combine(L, L.zst[0, k], L.zst[1, k]) for k in range(3)]
         c = combine(L, pz[r, 0], pz[r, 1]) + toward * own + along_y * cy + along_x * sideways
         c = jnp.where(zi < 2 * s * EQ * n, c, 0.0)
+        y_ends = L.zs[1] * jnp.where(my, L.yzs[...] * cy, 0.0)
         return (
             lambda side, e: rx[side][e],
             ry,
-            lambda e, i: unpack(L, c, e, i),
+            ends(L, L.zs[0] * c + y_ends),
         )
 
     def put(r, L, v):
@@ -339,9 +359,10 @@
 
     def deep(r, L):
         get = lambda e, i: field[r, e, i]
-        own = pack(L, get)
-        zpack[r, 0] = own
-        begin(plans[r]["d"], plans[r]["v"])
+        begin(plans[r]["d"], only=("xy",))
+        zpack[r, 0] = pack(L, get)
+        begin(plans[r]["d"], only=("xz", "yz"))
+        begin(plans[r]["v"])
         for e in every:
             for i in range(L.n):
                 pfield[r, e, i] = KEEP * get(e, i) + local(L, get, e, i)
@@ -350,7 +371,7 @@
 
         def finish():
             arrive(plans[r]["v"])
-            halo = received(L, r, hx, hy, hz)
+            halo = received(L, r, hx, hy, hz)[:3]
             new = planes(lambda e, i: border(L, pfield[r, e, i], halo, e, i), L)
 
             def outer():
@@ -425,16 +446,21 @@
     wargs = (wsend, wall, wr_sem)
 
     def everyone():
+        mirrored = all(count & (count - 1) == 0 for count in dims)
+
+        def other(index, step, count):
+            return index ^ step if mirrored else (index + step) % count
+
         made = []
-        for az in range(ngz):
-            for ay in range(ngy):
-                for ax in range(ngx):
+        for ay in reversed(range(ngy)):
+            for az in reversed(range(ngz)):
+                for ax in reversed(range(ngx)):
                     if ax + ay + az == 0:
                         continue
                     made.append(remote(
                         bsend.at[:, pl.ds(0, 1)], ball.at[X, core, :, pl.ds(row, 1)],
                         bs_sem, br_sem,
-                        ((gx + ax) % ngx, (gy + ay) % ngy, (gz + az) % ngz),
+                        (other(gx, ax, ngx), other(gy, ay, ngy), other(gz, az, ngz)),
                     ))
         return made
 
@@ -488,7 +514,7 @@
         L.zs[1] = pack(L, lambda e, i: L.st[e, 0, i])
         L.zs[2] = pack(L, lambda e, i: L.xw[e, 0 if i == 0 else 1], (0, L.n - 1))
 
-    loads[0].wait()
+    guess_load.wait()
     guess = lambda e, i: g_ref[e, i]
     zpack[0, 0] = pack(L0, guess)
     pl.semaphore_wait(barrier, awaited)
@@ -505,8 +531,7 @@
 
     if close:
         tell(0)
-    for load in loads[1:]:
-        load.wait()
+    await_rows(i_sem.at[1], 8 * EQ * nx * ny)
     level2 = [None] * (7 * EQ)
     for e in every:
         d1 = coarsen(d_ref[e], 1)
@@ -519,7 +544,7 @@
             c = scale(L1, lambda e, k, i: w1[6 * e + k, i], lambda e, i: d1[i], e, i)
             w1[6 * EQ + e, i] = c
     wsend[...] = to_rows(jnp.stack(level2))
-    own(wsend, wall, l_sem).start()
+    own(wsend, wall, i_sem.at[0]).start()
     start(0)
     for e in every:
         for i in range(nx):
@@ -535,10 +560,10 @@
         tell(1)
 
     arrive(plans[0]["v"])
-    halo = received(L0, 0, hx, hy, hz)
+    halo = received(L0, 0, hx, hy, hz)[:3]
     put(1, L0, planes(lambda e, i: border(L0, pfield[0, e, i], halo, e, i), L0))
     finish = deep(1, L0)
-    own(wsend, wall, l_sem).wait()
+    own(wsend, wall, i_sem.at[0]).wait()
     done(0)
     if close:
         pl.semaphore_wait(know.at[1], hear)
@@ -590,7 +615,7 @@
             r.append(L1.tot[e, i] * (total - DAMP * get(e, i)))
         rest.append(coarsen(jnp.stack(r), 2))
     bsend[...] = to_rows(jnp.stack(rest))
-    for copy in reversed(everyone()):
+    for copy in everyone():
         copy.start()
     own(bsend, ball, br_sem).start()
     zpack[3, 0] = pack(L1, lambda e, i: field[3, e, i])
@@ -709,6 +734,30 @@
             ]))
         return made
 
+    steps3 = ((-1, 0), (1, 0), (-2, 0), (2, 0), (0, -2), (0, 2))
+
+    def shifted(v, dr, dl):
+        return roll(roll(v, dl, 1), dr, 0)
+
+    def twice(w):
+        got = {(0, 0): KEEP * KEEP}
+
+        def add(at, value):
+            at = (at[0] % NY, at[1] % NZ)
+            got[at] = got[at] + value if at in got else value
+
+        for k, (dr, dl) in enumerate(steps3):
+            add((dr, dl), 2.0 * KEEP * w[k])
+            for m, (er, el) in enumerate(steps3):
+                if k == m and k < 2:
+                    continue
+                add((dr + er, dl + el), w[k] * shifted(w[m], dr, dl))
+        return got
+
+    def apply_twice(w, v):
+        turned = {dl: roll(v, dl, 1) for dl in sorted({at[1] for at in w})}
+        return tree([c * roll(turned[dl], dr, 0) for (dr, dl), c in w.items()])
+
     def inner(w, k, at, last, step):
         if k == 0 and step == 2:
             return jnp.where(even_y, w, 0.0) if at == last else w
@@ -728,7 +777,8 @@
                 weights[k].append(inner(scaled[at] * plain[k][at], k, at, count - 1, step))
         return scaled, totals, weights
 
-    c2, t2, w2, c3, w3 = [], [], [], [], []
+    c2, t2, w2, c3, w3, ww3 = [], [], [], [], [], []
+    by_two = pairs == 1 and NY >= 8 and COARSE_SWEEPS % 2 == 0
     for e in every:
         plain = [spread(wall, 6 * e + k) for k in range(6)]
         diagonal = spread(wall, 6 * EQ + e)
@@ -740,6 +790,8 @@
         scaled, _, weights = constants_of(coarse, halve(diagonal), pairs, 2)
         c3.append(scaled)
         w3.append(weights)
+        if by_two:
+            ww3.append(twice([weights[k][0] for k in range(6)]))
 
     arrive(plans[3]["v"])
     pltpu.make_async_copy(ball, ball, br_sem).wait()
@@ -764,11 +816,15 @@
         got = halve([t2[e][x] * ((rhs[e][x] - DAMP * v2[e][x]) + sums[x]) for x in range(NX)])
         rhs3.append([c3[e][p] * got[p] for p in range(pairs)])
     v3 = rhs3
-    for step in range(COARSE_SWEEPS - 1):
+    for step in range(1 if by_two else COARSE_SWEEPS - 1):
         sums = [around3(w3[e], v3[e]) for e in every]
         v3 = [
             [(KEEP * v3[e][p] + rhs3[e][p]) + sums[e][p] for p in range(pairs)] for e in every
         ]
+    if by_two:
+        once = v3
+        for step in range(COARSE_SWEEPS // 2 - 1):
+            v3 = [[apply_twice(ww3[e], v3[e][0]) + once[e][0]] for e in every]
     v2 = [[v2[e][x] + double(v3[e], x) for x in range(NX)] for e in every]
     for step in range(SWEEPS):
         v2 = smooth2(v2)
@@ -809,7 +865,7 @@
     def rows_y(kind, e, x):
         return jnp.where(yi < ny // 2, strip(kind, e, x, -1), strip(kind, e, x, qy))
 
-    left, behind, through = received(L1, 3, hx, hy, hz)
+    left, behind, _, columns = received(L1, 3, hx, hy, hz)
     mine = edge_rows(L1.s, *there["gy"])
 
     def add_x(side, e):
@@ -830,10 +886,10 @@
 
     def add_z(e, i):
         x = i // 2
-        got = through(e, i) + zco[e, 0, i] * plane(OUTSIDE_Z, e, x)
+        got = unpack(L1, columns, e, i) + zco[e, 0, i] * plane(OUTSIDE_Z, e, x)
         got = got + zco[e, 1, i] * across_x(OUTSIDE_Z, e, i)
         got = got + zco[e, 2, i] * across_y(OUTSIDE_Z, e, x)
-        return got + zco[e, 3, i] * plane(CENTER, e, x)
+        return L1.st[e, 1, i] * (got + zco[e, 3, i] * plane(CENTER, e, x))
 
     swept = pfield.at[3]
     for e in every:
@@ -888,7 +944,8 @@
             vmem((3, ny, nz), f32),
             vmem((2, EQ, ny, nz), f32),
             vmem((2, EQ, 2, ny, nz), f32),
-            vmem((EQ, 2, n, ny, nz), f32),
+            vmem((EQ, n, ny, nz), f32),
+            vmem((ny, nz), f32),
             vmem((EQ, 2, ny, nz), f32),
             vmem((2, 3, ny, nz), f32),
             dma,
@@ -938,14 +995,13 @@
             vmem((rows, nz), f32),
             vmem((ngx, ngy * qy, nz), f32),
             dma,
-            dma((rounds, 3)),
+            dma((4,)),
             dma,
             dma((4,)),
             dma((4,)),
             dma,
             dma,
-            dma,
-            dma((4,)),
+            dma((2,)),
             pltpu.SemaphoreType.REGULAR((2,)),
         ],
         compiler_params=pltpu.CompilerParams(

time: 25.8 us -> 25.3 us (0.981)
  Pallas kernels: 25 us -> 24.5 us
    pallas_call x1, Pallas kernels: 25 us -> 24.5 us  [per_device(): pl.pallas_call(functools.partial(kernel, dims, cores), out_shape=vmem(gue...]
where the time goes in v5:
time: 25.3 us; the launch traced here: 25.1 us
  Pallas kernels  24.5 us (97%)
  local copies, waits for them, and re-layouts  0.64 us (3%)
    pallas_call x1, Pallas kernels, per_device(): pl.pallas_call(functools.partial(kernel, dims, cores), out_shape=vmem(gue...  24.5 us
    unnamed x1, local copies, waits for them, and re-layouts  0.64 us

profile of v5, /device:TPU:0, one launch (start us, length us, event | category | flops | bytes accessed | tf_op | source)
XLA Modules:
  0.0 25.1 jit_solution(7212226162745546572)
XLA Ops:
  0.0 24.5 %shard_map.46 = f32[3,8,8,128]{3,2,1,0:T(8,128)S(1)} custom-call(f32[18,8,8,128]{3,2,1,0:T(8,128)} %w_hbm.1, f32[3,8,8,128]{3,2,1,0:T(8,128)} %d_hbm.1, f32[3,8,8,128]{3,2,1,0:T(8,128)} %b_hbm.1, f32[3,8,8,128]{3,2,1,0:T(8,128)} %g_hbm.1), custom_call_target="tpu_custom_call" | custom-call | tf_op jit(solution)/shard_map/pallas_call | solution.py:959
  24.5 0.6 %copy.6 = f32[3,8,8,128]{3,2,1,0:T(8,128)} copy(f32[3,8,8,128]{3,2,1,0:T(8,128)S(1)} %shard_map.46) | data formatting | bytes 196608

commit v6 on v5

--- a/solution.py
+++ b/solution.py
@@ -42,7 +42,7 @@
 ):
     level_refs = (rest[:13], rest[13:26])
     (wsend, wall, bsend, ball, e2, lines, broad, widen, mix, mixed,
-     s_sem, r_sem, co_sem, ws_sem, wr_sem, bs_sem, br_sem, i_sem, know) = rest[26:]
+     s_sem, r_sem, co_sem, ws_sem, wr_sem, bs_sem, br_sem, i_sem, g_sem, know) = rest[26:]
     ngx, ngy, ngz = dims
     nx, ny, nz = g_ref.shape[1:]
     half = nx // 2
@@ -64,8 +64,9 @@
         here.update(change)
         return (here["gx"], here["gy"], here["gz"])
 
-    guess_load = pltpu.make_async_copy(g_hbm, g_ref, i_sem.at[0])
-    guess_load.start()
+    guess_loads = [pltpu.make_async_copy(g_hbm.at[e], g_ref.at[e], g_sem.at[e]) for e in range(EQ)]
+    for load in guess_loads:
+        load.start()
     barrier = pltpu.get_barrier_semaphore()
     close = ngy <= 4 and ngz <= 4
     awaited = 0
@@ -403,10 +404,13 @@
     source = iota((nz, nz), 0)
     target = iota((nz, nz), 1)
     squeeze = jnp.where(source == 4 * (target % qz), 1.0, 0.0).astype(jnp.bfloat16)
-
-    def to_rows(a):
+    squeeze_pairs = jnp.where(
+        (source == 4 * (target % qz)) | (source == 4 * (target % qz) + 2), 1.0, 0.0
+    ).astype(jnp.bfloat16)
+
+    def to_rows(a, lanes):
         m = a.shape[0]
-        c = select(a.reshape(m * qx * ny, nz), squeeze).reshape(m, qx, ny, nz)
+        c = select(a.reshape(m * qx * ny, nz), lanes).reshape(m, qx, ny, nz)
         place = iota((m, ny, nz), 2) // qz
         got = jnp.zeros((m, ny, nz), jnp.float32)
         for x in range(qx):
@@ -514,7 +518,8 @@
         L.zs[1] = pack(L, lambda e, i: L.st[e, 0, i])
         L.zs[2] = pack(L, lambda e, i: L.xw[e, 0 if i == 0 else 1], (0, L.n - 1))
 
-    guess_load.wait()
+    for load in guess_loads:
+        load.wait()
     guess = lambda e, i: g_ref[e, i]
     zpack[0, 0] = pack(L0, guess)
     pl.semaphore_wait(barrier, awaited)
@@ -543,7 +548,7 @@
         for i in range(half):
             c = scale(L1, lambda e, k, i: w1[6 * e + k, i], lambda e, i: d1[i], e, i)
             w1[6 * EQ + e, i] = c
-    wsend[...] = to_rows(jnp.stack(level2))
+    wsend[...] = to_rows(jnp.stack(level2), squeeze)
     own(wsend, wall, i_sem.at[0]).start()
     start(0)
     for e in every:
@@ -613,8 +618,9 @@
             total = border(L1, q[e][i], halo, e, i)
             field[3, e, i] = KEEP * get(e, i) + total
             r.append(L1.tot[e, i] * (total - DAMP * get(e, i)))
-        rest.append(coarsen(jnp.stack(r), 2))
-    bsend[...] = to_rows(jnp.stack(rest))
+        r = [r[2 * x] + r[2 * x + 1] for x in range(qx)]
+        rest.append(jnp.stack([c + roll(c, -2, 0) for c in r]))
+    bsend[...] = 0.125 * to_rows(jnp.stack(rest), squeeze_pairs)
     for copy in everyone():
         copy.start()
     own(bsend, ball, br_sem).start()
@@ -1002,6 +1008,7 @@
             dma,
             dma,
             dma((2,)),
+            dma((3,)),
             pltpu.SemaphoreType.REGULAR((2,)),
         ],
         compiler_params=pltpu.CompilerParams(

time: 25.3 us -> 25 us (0.988)
  Pallas kernels: 24.5 us -> 24.2 us
where the time goes in v6:
time: 25 us; the launch traced here: 24.9 us
  Pallas kernels  24.2 us (97%)
  local copies, waits for them, and re-layouts  0.64 us (3%)
    pallas_call x1, Pallas kernels, per_device(): pl.pallas_call(functools.partial(kernel, dims, cores), out_shape=vmem(gue...  24.2 us
    unnamed x1, local copies, waits for them, and re-layouts  0.64 us

profile of v6, /device:TPU:0, one launch (start us, length us, event | category | flops | bytes accessed | tf_op | source)
XLA Modules:
  0.0 24.9 jit_solution(1109325096799058993)
XLA Ops:
  0.0 24.2 %shard_map.46 = f32[3,8,8,128]{3,2,1,0:T(8,128)S(1)} custom-call(f32[18,8,8,128]{3,2,1,0:T(8,128)} %w_hbm.1, f32[3,8,8,128]{3,2,1,0:T(8,128)} %d_hbm.1, f32[3,8,8,128]{3,2,1,0:T(8,128)} %b_hbm.1, f32[3,8,8,128]{3,2,1,0:T(8,128)} %g_hbm.1), custom_call_target="tpu_custom_call" | custom-call | tf_op jit(solution)/shard_map/pallas_call | solution.py:965
  24.2 0.6 %copy.6 = f32[3,8,8,128]{3,2,1,0:T(8,128)} copy(f32[3,8,8,128]{3,2,1,0:T(8,128)S(1)} %shard_map.46) | data formatting | bytes 196608

commit v7 on v6

--- a/solution.py
+++ b/solution.py
@@ -79,7 +79,7 @@
 
     for name, index, count in axes:
         if close and name != "gx":
-            steps = (-1, 1) if name == "gy" or cores == 1 else (-1, 1, -cores, cores)
+            steps = (-1, 1)
             for step in steps:
                 ok = (index + step >= 0) & (index + step < count)
                 awaited = awaited + greet(ok, device(**{name: jnp.clip(index + step, 0, count - 1)}))
@@ -524,15 +524,17 @@
     zpack[0, 0] = pack(L0, guess)
     pl.semaphore_wait(barrier, awaited)
     begin(plans[0]["v"])
-    hear = there["gy"][0].astype(jnp.int32) + there["gy"][1].astype(jnp.int32)
+    hear = found[0] + found[1] + found[2]
 
     def tell(k):
-        for side in range(2):
-            @pl.when(there["gy"][side])
-            def _():
-                pl.semaphore_signal(
-                    know.at[k], inc=1, device_id=device(gy=beside["gy"][side]), device_id_type=MESH
-                )
+        for name, _, _ in axes:
+            for side in range(2):
+                @pl.when(there[name][side])
+                def _():
+                    pl.semaphore_signal(
+                        know.at[k], inc=1, device_id=device(**{name: beside[name][side]}),
+                        device_id_type=MESH,
+                    )
 
     if close:
         tell(0)
@@ -567,11 +569,11 @@
     arrive(plans[0]["v"])
     halo = received(L0, 0, hx, hy, hz)[:3]
     put(1, L0, planes(lambda e, i: border(L0, pfield[0, e, i], halo, e, i), L0))
+    if close:
+        pl.semaphore_wait(know.at[1], hear)
     finish = deep(1, L0)
     own(wsend, wall, i_sem.at[0]).wait()
     done(0)
-    if close:
-        pl.semaphore_wait(know.at[1], hear)
     start(1)
     pack_constants(L1)
     begin(constants[1])

time: 25 us -> 24.9 us (level)
  no operation moved by 1% of the time
where the time goes in v7:
time: 24.9 us; the launch traced here: 24.8 us
  Pallas kernels  24.1 us (97%)
  local copies, waits for them, and re-layouts  0.64 us (3%)
    pallas_call x1, Pallas kernels, per_device(): pl.pallas_call(functools.partial(kernel, dims, cores), out_shape=vmem(gue...  24.1 us
    unnamed x1, local copies, waits for them, and re-layouts  0.64 us

profile of v7, /device:TPU:0, one launch (start us, length us, event | category | flops | bytes accessed | tf_op | source)
XLA Modules:
  0.0 24.8 jit_solution(10369963293147421111)
XLA Ops:
  0.0 24.1 %shard_map.46 = f32[3,8,8,128]{3,2,1,0:T(8,128)S(1)} custom-call(f32[18,8,8,128]{3,2,1,0:T(8,128)} %w_hbm.1, f32[3,8,8,128]{3,2,1,0:T(8,128)} %d_hbm.1, f32[3,8,8,128]{3,2,1,0:T(8,128)} %b_hbm.1, f32[3,8,8,128]{3,2,1,0:T(8,128)} %g_hbm.1), custom_call_target="tpu_custom_call" | custom-call | tf_op jit(solution)/shard_map/pallas_call | solution.py:967
  24.1 0.6 %copy.6 = f32[3,8,8,128]{3,2,1,0:T(8,128)} copy(f32[3,8,8,128]{3,2,1,0:T(8,128)S(1)} %shard_map.46) | data formatting | bytes 196608

commit v8 on v7

--- a/solution.py
+++ b/solution.py
@@ -524,10 +524,10 @@
     zpack[0, 0] = pack(L0, guess)
     pl.semaphore_wait(barrier, awaited)
     begin(plans[0]["v"])
-    hear = found[0] + found[1] + found[2]
+    hear = found[1] + found[2]
 
     def tell(k):
-        for name, _, _ in axes:
+        for name, _, _ in axes[1:]:
             for side in range(2):
                 @pl.when(there[name][side])
                 def _():

time: 24.9 us -> 24.9 us (level)
  no operation moved by 1% of the time
where the time goes in v8:
time: 24.9 us; the launch traced here: 24.7 us
  Pallas kernels  24.1 us (97%)
  local copies, waits for them, and re-layouts  0.64 us (3%)
    pallas_call x1, Pallas kernels, per_device(): pl.pallas_call(functools.partial(kernel, dims, cores), out_shape=vmem(gue...  24.1 us
    unnamed x1, local copies, waits for them, and re-layouts  0.64 us

profile of v8, /device:TPU:0, one launch (start us, length us, event | category | flops | bytes accessed | tf_op | source)
XLA Modules:
  0.0 24.7 jit_solution(4727345767874951116)
XLA Ops:
  0.0 24.1 %shard_map.46 = f32[3,8,8,128]{3,2,1,0:T(8,128)S(1)} custom-call(f32[18,8,8,128]{3,2,1,0:T(8,128)} %w_hbm.1, f32[3,8,8,128]{3,2,1,0:T(8,128)} %d_hbm.1, f32[3,8,8,128]{3,2,1,0:T(8,128)} %b_hbm.1, f32[3,8,8,128]{3,2,1,0:T(8,128)} %g_hbm.1), custom_call_target="tpu_custom_call" | custom-call | tf_op jit(solution)/shard_map/pallas_call | solution.py:967
  24.1 0.6 %copy.6 = f32[3,8,8,128]{3,2,1,0:T(8,128)} copy(f32[3,8,8,128]{3,2,1,0:T(8,128)S(1)} %shard_map.46) | data formatting | bytes 196608
